TPU v7x, 256 devices: a whole 4x4x8 slice. The times are simulated.
256 devices in a mesh: src: 4 (over z_hi), gx: 16 (over z_lo, y, core), gy: 4 (over x).
Axes of the slice: x: 4, y: 4, z: 8 (z_hi: 4, z_lo: 2; z = z_hi * 2 + z_lo), core: 2. Of those that a mesh axis runs over, the one named last changes fastest.
Arguments:
- adjoint_now: float32 [4, 2, 64, 128, 512], P('src', None, 'gx', 'gy'), may hold values from -6 to 6
- adjoint_before: float32 [4, 2, 64, 128, 512], P('src', None, 'gx', 'gy'), may hold values from -6 to 6
- forward_field: bfloat16 [3, 4, 2, 64, 128, 512], P(None, 'src', None, 'gx', 'gy'), may hold values from -6 to 6
- velocity: float32 [64, 128, 512], P('gx', 'gy'), may hold values from 0.2 to 0.4
- thomsen_eps: float32 [64, 128, 512], P('gx', 'gy'), may hold values from 0.05 to 0.35
- thomsen_delta: float32 [64, 128, 512], P('gx', 'gy'), may hold values from 0 to 0.25
- tilt_level: int32 [64, 128, 512], P('gx', 'gy'), may hold values from 0 to 31
- azimuth_level: int32 [64, 128, 512], P('gx', 'gy'), may hold values from 0 to 31
- channel_cell: int32 [4, 1536], P('src'), may hold values from 0 to 8191
- channel_count: int32 [4], P('src'), may hold values from 512 to 1536, as said below
- residual_trace: float32 [4, 3, 1536], P('src'), may hold values from -6 to 6
Outputs:
- adjoint_next: float32 [4, 2, 64, 128, 512], P('src', None, 'gx', 'gy')
- grad_velocity: float32 [64, 128, 512], P('gx', 'gy', 'src')
- grad_epsilon: float32 [64, 128, 512], P('gx', 'gy', 'src')
- grad_delta: float32 [64, 128, 512], P('gx', 'gy', 'src')
Inputs may be any that keep to these rules, and one draw needn't show every extreme that they name: `channel_count`: some virtual source has 1536 live channels and some other has 512.
All inputs are finite; a program needn't handle non-finite values.
Results may differ from a plain program's by a relative error of at most 0.0003.
Values sent between devices are 32-bit elements; how exact they have to be, the bound alone decides.
A program may use at most 64 MiB of HBM per device.

v0:
```python
import math

import jax
import jax.numpy as jnp
from jax import lax
from jax.sharding import PartitionSpec as P

LEVELS = 32


def extended_2(block, sides, width):
    for axis, dim in sides:
        count = lax.axis_size(axis)
        forward = [(i, i + 1) for i in range(count - 1)]
        backward = [(target, source) for source, target in forward]
        low = lax.ppermute(
            lax.slice_in_dim(block, block.shape[dim] - width, None, axis=dim), axis, forward
        )
        high = lax.ppermute(lax.slice_in_dim(block, 0, width, axis=dim), axis, backward)
        block = jnp.concatenate([low, block, high], axis=dim)
    return block


def derivatives(padded):
    center = padded[..., 1:-1, 1:-1, 1:-1]
    second_x = padded[..., 2:, 1:-1, 1:-1] + padded[..., :-2, 1:-1, 1:-1] - 2.0 * center
    second_y = padded[..., 1:-1, 2:, 1:-1] + padded[..., 1:-1, :-2, 1:-1] - 2.0 * center
    second_z = padded[..., 1:-1, 1:-1, 2:] + padded[..., 1:-1, 1:-1, :-2] - 2.0 * center
    mixed_xy = 0.25 * (
        padded[..., 2:, 2:, 1:-1]
        - padded[..., 2:, :-2, 1:-1]
        - padded[..., :-2, 2:, 1:-1]
        + padded[..., :-2, :-2, 1:-1]
    )
    mixed_yz = 0.25 * (
        padded[..., 1:-1, 2:, 2:]
        - padded[..., 1:-1, 2:, :-2]
        - padded[..., 1:-1, :-2, 2:]
        + padded[..., 1:-1, :-2, :-2]
    )
    mixed_xz = 0.25 * (
        padded[..., 2:, 1:-1, 2:]
        - padded[..., 2:, 1:-1, :-2]
        - padded[..., :-2, 1:-1, 2:]
        + padded[..., :-2, 1:-1, :-2]
    )
    return (second_x, second_y, second_z, mixed_xy, mixed_yz, mixed_xz)


def tilt_weights(tilt_level, azimuth_level):
    theta = tilt_level.astype(jnp.float32) * (0.5 * math.pi / LEVELS)
    azimuth = azimuth_level.astype(jnp.float32) * (2.0 * math.pi / LEVELS)
    sin_t = jnp.sin(theta)
    cos_t = jnp.cos(theta)
    sin_p = jnp.sin(azimuth)
    cos_p = jnp.cos(azimuth)
    return (
        sin_t * sin_t * cos_p * cos_p,
        sin_t * sin_t * sin_p * sin_p,
        cos_t * cos_t,
        2.0 * sin_t * sin_t * sin_p * cos_p,
        2.0 * sin_t * cos_t * sin_p,
        2.0 * sin_t * cos_t * cos_p,
    )


def split_operators(padded, weights):
    parts = derivatives(padded)
    axial = weights[0] * parts[0]
    for index in range(1, 6):
        axial = axial + weights[index] * parts[index]
    laplace = parts[0] + parts[1] + parts[2]
    return (laplace[..., 0, :, :, :] - axial[..., 0, :, :, :], axial[..., 1, :, :, :])


def exchange_rims(current):
    return extended_2(current, (("gx", 2), ("gy", 3)), 1)


def on_device(
    adjoint_now,
    adjoint_before,
    forward_field,
    velocity,
    thomsen_eps,
    thomsen_delta,
    tilt_level,
    azimuth_level,
    channel_cell,
    channel_count,
    residual_trace,
):
    tile_x, tile_y, depth = velocity.shape
    sources_here = adjoint_now.shape[0]
    step_count = forward_field.shape[0]
    width_y = tile_y * lax.axis_size("gy")
    start_x = lax.axis_index("gx") * tile_x
    start_y = lax.axis_index("gy") * tile_y
    local_x = channel_cell // width_y - start_x
    local_y = channel_cell % width_y - start_y
    slots = lax.broadcasted_iota(jnp.int32, channel_cell.shape, 1)
    inside = (
        (local_x >= 0)
        & (local_x < tile_x)
        & (local_y >= 0)
        & (local_y < tile_y)
        & (slots < channel_count[:, None])
    )
    target = jnp.where(inside, local_x * tile_y + local_y, -1)
    cells = jnp.arange(tile_x * tile_y, dtype=jnp.int32)
    onehot = (target[:, :, None] == cells[None, None, :]).astype(jnp.float32)
    surface = jnp.einsum("stc,scm->stm", residual_trace, onehot, precision=lax.Precision.HIGHEST)
    surface = surface.reshape(sources_here, step_count, tile_x, tile_y)
    weights = tilt_weights(tilt_level, azimuth_level)
    speed_sq = velocity * velocity
    stretch = 1.0 + 2.0 * thomsen_eps
    root = jnp.sqrt(1.0 + 2.0 * thomsen_delta)
    share_velocity = None
    total_velocity = jnp.zeros_like(velocity)
    total_epsilon = jnp.zeros_like(velocity)
    total_delta = jnp.zeros_like(velocity)
    current = adjoint_now
    previous = adjoint_before
    for time_step in range(step_count):
        extended = exchange_rims(current)
        padded = jnp.pad(extended, ((0, 0), (0, 0), (0, 0), (0, 0), (1, 1)))
        horiz_p, axial_q = split_operators(padded, weights)
        update_p = stretch * horiz_p + root * axial_q
        update_q = root * horiz_p + axial_q
        following = 2.0 * current - previous + speed_sq * jnp.stack([update_p, update_q], axis=1)
        following = following.at[:, 0, :, :, 0].add(surface[:, time_step])
        forward_p = forward_field[time_step, :, 0].astype(jnp.float32)
        forward_q = forward_field[time_step, :, 1].astype(jnp.float32)
        term_velocity = jnp.sum(
            2.0 * velocity * (forward_p * update_p + forward_q * update_q), axis=0
        )
        term_epsilon = jnp.sum(2.0 * speed_sq * forward_p * horiz_p, axis=0)
        term_delta = jnp.sum(speed_sq / root * (forward_p * axial_q + forward_q * horiz_p), axis=0)
        total_velocity = total_velocity + term_velocity
        total_epsilon = total_epsilon + term_epsilon
        total_delta = total_delta + term_delta
        previous = current
        current = following
    share_velocity, share_epsilon, share_delta = (
        lax.psum_scatter(total_velocity, "src", scatter_dimension=2, tiled=True),
        lax.psum_scatter(total_epsilon, "src", scatter_dimension=2, tiled=True),
        lax.psum_scatter(total_delta, "src", scatter_dimension=2, tiled=True),
    )
    return (current, share_velocity, share_epsilon, share_delta)


def solution(mesh):
    placed = (
        P("src", None, "gx", "gy", None),
        P("src", None, "gx", "gy", None),
        P(None, "src", None, "gx", "gy", None),
        P("gx", "gy", None),
        P("gx", "gy", None),
        P("gx", "gy", None),
        P("gx", "gy", None),
        P("gx", "gy", None),
        P("src", None),
        P("src"),
        P("src", None, None),
    )
    return jax.shard_map(
        on_device,
        mesh=mesh,
        in_specs=placed,
        out_specs=(
            P("src", None, "gx", "gy", None),
            P("gx", "gy", "src"),
            P("gx", "gy", "src"),
            P("gx", "gy", "src"),
        ),
        check_vma=False,
    )
```

profile of v0, /device:TPU:32, one launch (start us, length us, event | category | flops | bytes accessed | tf_op | source)
XLA Modules:
  0.0 236.1 jit_solution(12843129055211640923)
XLA Ops:
  7.2 1.0 fusion.95
  8.2 1.9 collective-permute-start.1
  10.2 5.8 %collective-permute-start = (f32[1,2,1,32,512]{4,3,2,1,0:T(8,128)S(1)}, f32[1,2,1,32,512]{4,3,2,1,0:T(8,128)S(1)}, u32[]{:S(2)}, u32[]{:S(2)}) collective-permute-start(f32[1,2,1,32,512]{4,3,2,1,0:T(8,128)S(1)} %get-tuple-element.103), channel_id=1, source_target_pairs={{4,0},{8,4},{12,8},{16,12},{20,16},{24,20},{28,24},{32,28},{36,32}... | collective-permute-start | bytes 393224 | tf_op jit(solution)/shard_map/ppermute | solution.py:19
  16.6 3.4 %multiply_multiply_fusion.1 = (f32[4,32,512]{2,1,0:T(8,128)S(1)}, f32[4,32,512]{2,1,0:T(8,128)S(1)}, f32[4,32,512]{2,1,0:T(8,128)S(1)}, f32[4,32,512]{2,1,0:T(8,...) fusion(s32[4,32,512]{2,1,0:T(8,128)} %param.24, s32[4,32,512]{2,1,0:T(8,128)} %param.23), kind=kLoop, calls=%fused_computation.120 | loop fusion | flops 1310720 | bytes 2097152 | tf_op jit(solution)/shard_map/mul | solution.py:58
  20.2 0.5 convolution_bitcast_fusion
  20.9 0.8 copy.264
  21.7 1.3 collective-permute-start.2
  22.9 0.6 copy.265
  23.6 5.1 %collective-permute-start.3 = (f32[1,2,6,1,512]{4,1,3,2,0:T(2,128)}, f32[1,2,6,1,512]{4,1,3,2,0:T(2,128)}, u32[]{:S(2)}, u32[]{:S(2)}) collective-permute-start(f32[1,2,6,1,512]{4,1,3,2,0:T(2,128)} %copy.265), channel_id=1, source_target_pairs={{0,1},{1,2},{2,3},{4,5},{5,6},{6,7},{8,9},{9,10},{10,11},{12,13},{... | collective-permute-start | bytes 73736 | tf_op jit(solution)/shard_map/ppermute | solution.py:16
  28.7 0.6 slice_bitcast_fusion.3
  29.3 1.4 copy.242
  30.8 0.8 copy.237
  31.6 0.8 copy.239
  32.3 0.6 select_maximum_fusion.8
  33.0 3.8 %fusion.10 = (f32[1,2,4,32,512]{4,3,2,1,0:T(8,128)S(1)}, f32[1,2,4,32,512]{4,3,2,1,0:T(8,128)S(1)}, f32[1,2,4,32,512]{4,3,2,1,0:T(8,128)S(1)}, f32[1,2,4,32,512]{4,3,2,1,0:T(8,128)S(1)}) fusion(f32[1,2,6,32,512]{4,3,2,1,0:T(8,128)} %copy-done.23, f32[1,2,6,1,512]{4,3,2,1,0:T(1,128)S(1)} %copy.239, f32[1,2,6,1,512]{4,3,2,1,0:T(1,128)S(1)} %copy.237, ...), kind=kLoop, calls=%fused_computation.35 | loop fusion | flops 4587520 | bytes 10534912 | tf_op jit(solution)/shard_map/add | solution.py:71
  36.8 0.2 multiply_add_fusion.5
  37.1 0.7 copy-done.36
  37.8 0.2 fusion.41
  38.1 0.1 scatter-add.10
  38.2 2.9 %collective-permute-start.4 = (f32[1,2,1,32,512]{4,3,2,1,0:T(8,128)S(1)}, f32[1,2,1,32,512]{4,3,2,1,0:T(8,128)S(1)}, u32[]{:S(2)}, u32[]{:S(2)}) collective-permute-start(f32[1,2,1,32,512]{4,3,2,1,0:T(8,128)S(1)} %get-tuple-element.97), channel_id=1, source_target_pairs={{4,0},{8,4},{12,8},{16,12},{20,16},{24,20},{28,24},{32,28},{36,32}... | collective-permute-start | bytes 393224 | tf_op jit(solution)/shard_map/ppermute | solution.py:19
  41.1 1.9 collective-permute-start.5
  43.1 0.6 collective-permute-done.4
  43.6 5.9 %collective-permute-done.5 = f32[1,2,1,32,512]{4,3,2,1,0:T(8,128)S(1)} collective-permute-done((f32[1,2,1,32,512]{4,3,2,1,0:T(8,128)S(1)}, f32[1,2,1,32,512]{4,3,2,1,0:T(8,128)S(1)}, u32[]{:S(2)}, u32[]{:S(2)}) %collective-permute-start.5) | collective-permute-done | bytes 131104 | tf_op jit(solution)/shard_map/ppermute | solution.py:16
  49.6 1.3 collective-permute-start.6
  50.9 4.5 %collective-permute-start.7 = (f32[1,2,6,1,512]{4,1,3,2,0:T(2,128)S(1)}, f32[1,2,6,1,512]{4,1,3,2,0:T(2,128)S(1)}, u32[]{:S(2)}, u32[]{:S(2)}) collective-permute-start(f32[1,2,6,1,512]{4,1,3,2,0:T(2,128)S(1)} %copy.245), channel_id=1, source_target_pairs={{0,1},{1,2},{2,3},{4,5},{5,6},{6,7},{8,9},{9,10},{10,11},{12,13},{... | collective-permute-start | bytes 73736 | tf_op jit(solution)/shard_map/ppermute | solution.py:16
  55.5 0.1 copy.249
  55.6 1.4 collective-permute-done.7
  57.0 0.2 pad_maximum_fusion
  57.3 0.5 select_maximum_fusion.4
  57.8 0.3 copy-done.9
  58.5 1.1 fusion.27
  59.6 0.2 multiply_add_fusion.3
  59.9 0.4 copy-done.3
  60.4 0.2 fusion.42
  60.6 0.1 scatter-add.11
  60.8 1.9 collective-permute-start.8
  62.7 2.4 %collective-permute-start.9 = (f32[1,2,1,32,512]{4,3,2,1,0:T(8,128)S(1)}, f32[1,2,1,32,512]{4,3,2,1,0:T(8,128)S(1)}, u32[]{:S(2)}, u32[]{:S(2)}) collective-permute-start(f32[1,2,1,32,512]{4,3,2,1,0:T(8,128)S(1)} %get-tuple-element.94), channel_id=1, source_target_pairs={{0,4},{4,8},{8,12},{12,16},{16,20},{20,24},{24,28},{28,32},{32,36}... | collective-permute-start | bytes 393224 | tf_op jit(solution)/shard_map/ppermute | solution.py:16
  65.2 5.9 %collective-permute-done.9 = f32[1,2,1,32,512]{4,3,2,1,0:T(8,128)S(1)} collective-permute-done((f32[1,2,1,32,512]{4,3,2,1,0:T(8,128)S(1)}, f32[1,2,1,32,512]{4,3,2,1,0:T(8,128)S(1)}, u32[]{:S(2)}, u32[]{:S(2)}) %collective-permute-start.9) | collective-permute-done | bytes 131104 | tf_op jit(solution)/shard_map/ppermute | solution.py:16
  71.2 1.3 collective-permute-start.10
  72.5 5.0 %collective-permute-start.11 = (f32[1,2,6,1,512]{4,1,3,2,0:T(2,128)S(1)}, f32[1,2,6,1,512]{4,1,3,2,0:T(2,128)S(1)}, u32[]{:S(2)}, u32[]{:S(2)}) collective-permute-start(f32[1,2,6,1,512]{4,1,3,2,0:T(2,128)S(1)} %copy.252), channel_id=1, source_target_pairs={{0,1},{1,2},{2,3},{4,5},{5,6},{6,7},{8,9},{9,10},{10,11},{12,13},{... | collective-permute-start | bytes 73736 | tf_op jit(solution)/shard_map/ppermute | solution.py:16
  77.6 1.3 collective-permute-done.11
  78.9 0.2 pad_maximum_fusion.1
  79.2 0.5 select_maximum_fusion
  79.7 0.3 copy-done.7
  80.5 1.1 fusion.17
  81.5 0.2 copy-done.5
  81.8 1.1 fusion.52
  82.9 0.9 fusion.62
  83.9 0.2 copy-done.30
  84.1 1.2 fusion.48
  85.2 2.4 %copy.258 = f32[4,32,512]{1,0,2:T(4,128)} copy(f32[4,32,512]{2,1,0:T(8,128)} %fusion.62) | data formatting | bytes 524288 | tf_op jit(solution)/shard_map/add | solution.py:140
  87.6 1.3 copy.257
  89.0 1.3 copy.259
  90.4 0.1 copy.256
  90.5 0.5 copy-done.40
  91.0 0.6 dynamic-slice.21
  92.2 0.2 fusion.43
  92.5 0.1 scatter-add.14
  92.6 132.4 %all-reduce.9.cloned.1.call-done = (f32[4,32,512]{1,0,2:T(4,128)}, f32[4,32,512]{1,0,2:T(4,128)}, f32[4,32,512]{1,0,2:T(4,128)}) async-done(((f32[4,32,512]{1,0,2:T(4,128)}, f32[4,32,512]{1,0,2:T(4,128)}, f32[4,32,512]{1,0,2:T(4,128)}), (f32[4,32,512]{1,0,2:T(4,128)}, f32[4,32,512]{1,0,2:T(4,128)}, f32[4,32,512]{1,0,2:T(4,128)})) %all-reduce.9.cloned.1.call-update) | async-done | bytes 786448
  225.0 1.1 constant_dynamic-slice_fusion
  226.1 0.7 copy.261
  226.8 0.7 copy.262
  227.6 1.0 constant_dynamic-slice_fusion.2
  228.5 0.7 copy.260
  (108 shorter events, 2.0 us)
Async XLA Ops:
  7.2 12.9 %copy-start.38 = (s32[1,1536]{1,0:T(1,128)S(1)}, s32[1,1536]{1,0:T(1,128)}, u32[]{:S(2)}) copy-start(s32[1,1536]{1,0:T(1,128)} %param.25) | copy-start | bytes 18436
  7.2 13.0 %copy-start.39 = (f32[1,3,1536]{2,0,1:T(1,128)S(1)}, f32[1,3,1536]{2,0,1:T(1,128)}, u32[]{:S(2)}) copy-start(f32[1,3,1536]{2,0,1:T(1,128)} %param.27) | copy-start | bytes 55300
  7.2 217.8 %all-reduce.9.cloned.1.call-start = ((), (), s32[]{:S(2)}) async-start(), calls=%async_computation | async-start | bytes 6291456
  8.2 12.5 %collective-permute-start.1 = (f32[1,2,1,32,512]{4,3,2,1,0:T(8,128)S(1)}, f32[1,2,1,32,512]{4,3,2,1,0:T(8,128)S(1)}, u32[]{:S(2)}, u32[]{:S(2)}) collective-permute-start(f32[1,2,1,32,512]{4,3,2,1,0:T(8,128)S(1)} %get-tuple-element.104), channel_id=1, source_target_pairs={{0,4},{4,8},{8,12},{12,16},{16,20},{20,24},{24,28},{28,32},{32,36}... | collective-permute-start | bytes 393224 | tf_op jit(solution)/shard_map/ppermute | solution.py:16
  10.2 10.7 %collective-permute-start = (f32[1,2,1,32,512]{4,3,2,1,0:T(8,128)S(1)}, f32[1,2,1,32,512]{4,3,2,1,0:T(8,128)S(1)}, u32[]{:S(2)}, u32[]{:S(2)}) collective-permute-start(f32[1,2,1,32,512]{4,3,2,1,0:T(8,128)S(1)} %get-tuple-element.103), channel_id=1, source_target_pairs={{4,0},{8,4},{12,8},{16,12},{20,16},{24,20},{28,24},{32,28},{36,32}... | collective-permute-start | bytes 393224 | tf_op jit(solution)/shard_map/ppermute | solution.py:19
  16.6 4.2 %copy-start = (f32[1,2,4,32,512]{4,3,2,1,0:T(8,128)S(1)}, f32[1,2,4,32,512]{4,3,2,1,0:T(8,128)}, u32[]{:S(2)}) copy-start(f32[1,2,4,32,512]{4,3,2,1,0:T(8,128)} %param.17) | copy-start | bytes 1572868
  20.0 13.0 %copy-start.8 = (f32[4,32,512]{2,1,0:T(8,128)}, f32[4,32,512]{2,1,0:T(8,128)S(1)}, u32[]{:S(2)}) copy-start(f32[4,32,512]{2,1,0:T(8,128)S(1)} %get-tuple-element.99) | copy-start | bytes 786436
  20.0 13.0 %copy-start.11 = (f32[4,32,512]{2,1,0:T(8,128)}, f32[4,32,512]{2,1,0:T(8,128)S(1)}, u32[]{:S(2)}) copy-start(f32[4,32,512]{2,1,0:T(8,128)S(1)} %get-tuple-element.100) | copy-start | bytes 786436
  20.0 13.0 %copy-start.14 = (f32[4,32,512]{2,1,0:T(8,128)}, f32[4,32,512]{2,1,0:T(8,128)S(1)}, u32[]{:S(2)}) copy-start(f32[4,32,512]{2,1,0:T(8,128)S(1)} %get-tuple-element.101) | copy-start | bytes 786436
  20.0 13.0 %copy-start.17 = (f32[4,32,512]{2,1,0:T(8,128)}, f32[4,32,512]{2,1,0:T(8,128)S(1)}, u32[]{:S(2)}) copy-start(f32[4,32,512]{2,1,0:T(8,128)S(1)} %get-tuple-element.102) | copy-start | bytes 786436
  20.0 13.0 %copy-start.20 = (f32[4,32,512]{2,1,0:T(8,128)}, f32[4,32,512]{2,1,0:T(8,128)S(1)}, u32[]{:S(2)}) copy-start(f32[4,32,512]{2,1,0:T(8,128)S(1)} %get-tuple-element.105) | copy-start | bytes 786436
  20.0 37.8 %copy-start.6 = (f32[4,32,512]{2,1,0:T(8,128)}, f32[4,32,512]{2,1,0:T(8,128)S(1)}, u32[]{:S(2)}) copy-start(f32[4,32,512]{2,1,0:T(8,128)S(1)} %get-tuple-element.98) | copy-start | bytes 786436
  20.0 9.3 %copy-start.2 = (f32[4,32,512]{2,1,0:T(8,128)S(1)}, f32[4,32,512]{2,1,0:T(8,128)}, u32[]{:S(2)}) copy-start(f32[4,32,512]{2,1,0:T(8,128)} %param.20) | copy-start | bytes 786436
  20.8 7.9 %copy-start.34 = (f32[1,2,1,32,512]{4,3,2,1,0:T(8,128)}, f32[1,2,1,32,512]{4,3,2,1,0:T(8,128)S(1)}, u32[]{:S(2)}) copy-start(f32[1,2,1,32,512]{4,3,2,1,0:T(8,128)S(1)} %collective-permute-done) | copy-start | bytes 393220
  20.9 12.1 %copy-start.23 = (f32[1,2,6,32,512]{4,3,2,1,0:T(8,128)}, f32[1,2,6,32,512]{4,3,2,1,0:T(8,128)S(1)}, u32[]{:S(2)}) copy-start(f32[1,2,6,32,512]{4,3,2,1,0:T(8,128)S(1)} %constant_dynamic-update-slice_fusion) | copy-start | bytes 2359300
  21.7 9.1 %collective-permute-start.2 = (f32[1,2,6,1,512]{4,1,3,2,0:T(2,128)}, f32[1,2,6,1,512]{4,1,3,2,0:T(2,128)}, u32[]{:S(2)}, u32[]{:S(2)}) collective-permute-start(f32[1,2,6,1,512]{4,1,3,2,0:T(2,128)} %copy.264), channel_id=1, source_target_pairs={{1,0},{2,1},{3,2},{5,4},{6,5},{7,6},{9,8},{10,9},{11,10},{13,12},{... | collective-permute-start | bytes 73736 | tf_op jit(solution)/shard_map/ppermute | solution.py:19
  23.6 8.0 %collective-permute-start.3 = (f32[1,2,6,1,512]{4,1,3,2,0:T(2,128)}, f32[1,2,6,1,512]{4,1,3,2,0:T(2,128)}, u32[]{:S(2)}, u32[]{:S(2)}) collective-permute-start(f32[1,2,6,1,512]{4,1,3,2,0:T(2,128)} %copy.265), channel_id=1, source_target_pairs={{0,1},{1,2},{2,3},{4,5},{5,6},{6,7},{8,9},{9,10},{10,11},{12,13},{... | collective-permute-start | bytes 73736 | tf_op jit(solution)/shard_map/ppermute | solution.py:16
  30.8 2.2 copy-start.35
  33.0 3.8 %copy-start.1 = (f32[4,32,512]{2,1,0:T(8,128)S(1)}, f32[4,32,512]{2,1,0:T(8,128)}, u32[]{:S(2)}) copy-start(f32[4,32,512]{2,1,0:T(8,128)} %param.22) | copy-start | bytes 786436
  33.0 3.8 %copy-start.24 = (f32[4,32,512]{2,1,0:T(8,128)S(1)}, f32[4,32,512]{2,1,0:T(8,128)}, u32[]{:S(2)}) copy-start(f32[4,32,512]{2,1,0:T(8,128)} %param.21) | copy-start | bytes 786436
  36.8 1.0 copy-start.36
  37.0 1.0 copy-start.27
  37.1 0.9 copy-start.37
  38.2 5.4 %collective-permute-start.4 = (f32[1,2,1,32,512]{4,3,2,1,0:T(8,128)S(1)}, f32[1,2,1,32,512]{4,3,2,1,0:T(8,128)S(1)}, u32[]{:S(2)}, u32[]{:S(2)}) collective-permute-start(f32[1,2,1,32,512]{4,3,2,1,0:T(8,128)S(1)} %get-tuple-element.97), channel_id=1, source_target_pairs={{4,0},{8,4},{12,8},{16,12},{20,16},{24,20},{28,24},{32,28},{36,32}... | collective-permute-start | bytes 393224 | tf_op jit(solution)/shard_map/ppermute | solution.py:19
  41.1 8.4 %collective-permute-start.5 = (f32[1,2,1,32,512]{4,3,2,1,0:T(8,128)S(1)}, f32[1,2,1,32,512]{4,3,2,1,0:T(8,128)S(1)}, u32[]{:S(2)}, u32[]{:S(2)}) collective-permute-start(f32[1,2,1,32,512]{4,3,2,1,0:T(8,128)S(1)} %get-tuple-element.96), channel_id=1, source_target_pairs={{0,4},{4,8},{8,12},{12,16},{16,20},{20,24},{24,28},{28,32},{32,36}... | collective-permute-start | bytes 393224 | tf_op jit(solution)/shard_map/ppermute | solution.py:16
  49.6 6.0 %collective-permute-start.6 = (f32[1,2,6,1,512]{4,1,3,2,0:T(2,128)S(1)}, f32[1,2,6,1,512]{4,1,3,2,0:T(2,128)S(1)}, u32[]{:S(2)}, u32[]{:S(2)}) collective-permute-start(f32[1,2,6,1,512]{4,1,3,2,0:T(2,128)S(1)} %copy.243), channel_id=1, source_target_pairs={{1,0},{2,1},{3,2},{5,4},{6,5},{7,6},{9,8},{10,9},{11,10},{13,12},{... | collective-permute-start | bytes 73736 | tf_op jit(solution)/shard_map/ppermute | solution.py:19
  50.9 6.1 %collective-permute-start.7 = (f32[1,2,6,1,512]{4,1,3,2,0:T(2,128)S(1)}, f32[1,2,6,1,512]{4,1,3,2,0:T(2,128)S(1)}, u32[]{:S(2)}, u32[]{:S(2)}) collective-permute-start(f32[1,2,6,1,512]{4,1,3,2,0:T(2,128)S(1)} %copy.245), channel_id=1, source_target_pairs={{0,1},{1,2},{2,3},{4,5},{5,6},{6,7},{8,9},{9,10},{10,11},{12,13},{... | collective-permute-start | bytes 73736 | tf_op jit(solution)/shard_map/ppermute | solution.py:16
  57.2 1.0 copy-start.9
  57.2 1.0 copy-start.12
  57.3 1.1 copy-start.15
  57.3 1.2 copy-start.18
  57.3 1.2 copy-start.21
  58.5 1.1 copy-start.25
  59.6 0.8 copy-start.3
  59.8 0.8 copy-start.29
  60.8 4.4 %collective-permute-start.8 = (f32[1,2,1,32,512]{4,3,2,1,0:T(8,128)S(1)}, f32[1,2,1,32,512]{4,3,2,1,0:T(8,128)S(1)}, u32[]{:S(2)}, u32[]{:S(2)}) collective-permute-start(f32[1,2,1,32,512]{4,3,2,1,0:T(8,128)S(1)} %get-tuple-element.95), channel_id=1, source_target_pairs={{4,0},{8,4},{12,8},{16,12},{20,16},{24,20},{28,24},{32,28},{36,32}... | collective-permute-start | bytes 393224 | tf_op jit(solution)/shard_map/ppermute | solution.py:19
  62.7 8.4 %collective-permute-start.9 = (f32[1,2,1,32,512]{4,3,2,1,0:T(8,128)S(1)}, f32[1,2,1,32,512]{4,3,2,1,0:T(8,128)S(1)}, u32[]{:S(2)}, u32[]{:S(2)}) collective-permute-start(f32[1,2,1,32,512]{4,3,2,1,0:T(8,128)S(1)} %get-tuple-element.94), channel_id=1, source_target_pairs={{0,4},{4,8},{8,12},{12,16},{16,20},{20,24},{24,28},{28,32},{32,36}... | collective-permute-start | bytes 393224 | tf_op jit(solution)/shard_map/ppermute | solution.py:16
  71.2 6.4 %collective-permute-start.10 = (f32[1,2,6,1,512]{4,1,3,2,0:T(2,128)S(1)}, f32[1,2,6,1,512]{4,1,3,2,0:T(2,128)S(1)}, u32[]{:S(2)}, u32[]{:S(2)}) collective-permute-start(f32[1,2,6,1,512]{4,1,3,2,0:T(2,128)S(1)} %copy.250), channel_id=1, source_target_pairs={{1,0},{2,1},{3,2},{5,4},{6,5},{7,6},{9,8},{10,9},{11,10},{13,12},{... | collective-permute-start | bytes 73736 | tf_op jit(solution)/shard_map/ppermute | solution.py:19
  72.5 6.3 %collective-permute-start.11 = (f32[1,2,6,1,512]{4,1,3,2,0:T(2,128)S(1)}, f32[1,2,6,1,512]{4,1,3,2,0:T(2,128)S(1)}, u32[]{:S(2)}, u32[]{:S(2)}) collective-permute-start(f32[1,2,6,1,512]{4,1,3,2,0:T(2,128)S(1)} %copy.252), channel_id=1, source_target_pairs={{0,1},{1,2},{2,3},{4,5},{5,6},{6,7},{8,9},{9,10},{10,11},{12,13},{... | collective-permute-start | bytes 73736 | tf_op jit(solution)/shard_map/ppermute | solution.py:16
  79.1 1.0 copy-start.7
  79.1 1.0 copy-start.10
  79.1 1.1 copy-start.13
  79.1 1.2 copy-start.16
  79.1 1.2 copy-start.19
  79.1 1.3 copy-start.22
  80.5 1.1 copy-start.4
  80.5 1.3 copy-start.5
  82.9 0.9 copy-start.26
  82.9 1.0 copy-start.28
  82.9 1.2 copy-start.30
  85.2 2.4 %copy-start.32 = (f32[4,32,512]{2,1,0:T(8,128)S(1)}, f32[4,32,512]{2,1,0:T(8,128)}, u32[]{:S(2)}) copy-start(f32[4,32,512]{2,1,0:T(8,128)} %get-tuple-element.65) | copy-start | bytes 786436
  85.2 3.7 %copy-start.31 = (f32[4,32,512]{2,1,0:T(8,128)S(1)}, f32[4,32,512]{2,1,0:T(8,128)}, u32[]{:S(2)}) copy-start(f32[4,32,512]{2,1,0:T(8,128)} %get-tuple-element.63) | copy-start | bytes 786436
  90.3 0.7 copy-start.40
  92.6 136.7 %copy-start.33 = (f32[1,2,4,32,512]{4,3,2,1,0:T(8,128)}, f32[1,2,4,32,512]{4,3,2,1,0:T(8,128)S(1)}, u32[]{:S(2)}) copy-start(f32[1,2,4,32,512]{4,3,2,1,0:T(8,128)S(1)} %scatter-add.14) | copy-start | bytes 1572868
Sparse Core Ops, SparseCore 0:
  90.5 134.4 all-reduce.8
where the time goes:
time: 239 us; the launch traced here: 236 us
  waiting for transfers between devices  148 us (62%)
  starting transfers between devices  35.4 us (15%)
  local copies, waits for them, and re-layouts  20.6 us (9%)
  between operations  16.1 us (7%)
  other arithmetic  16 us (7%)
    unnamed x2, waiting for transfers between devices  132 us
    ppermute x6, starting transfers between devices, extended_2(): lax.ppermute(lax.slice_in_dim(block, block.shape[dim] - width, None, axis...  21 us
    ppermute x6, starting transfers between devices, extended_2(): lax.ppermute(lax.slice_in_dim(block, 0, width, axis=dim), axis, backward)  14.4 us
    ppermute x6, waiting for transfers between devices, extended_2(): lax.ppermute(lax.slice_in_dim(block, block.shape[dim] - width, None, axis...  14.4 us
    unnamed x92, local copies, waits for them, and re-layouts  10 us
    add x3, other arithmetic, split_operators(): axial = axial + weights[index] * parts[index]  5.88 us
  transfers between devices with their start and end apart: 13, of which 7 were waited for; matrix products, arithmetic and copies ran while one was open for 4% of the time, Pallas kernels for 0%

commit v1 on v0

v1 whole, which is shorter than its diff:
```python
import functools
import math

import jax
import jax.numpy as jnp
from jax import lax
from jax.experimental import pallas as pl
from jax.experimental.pallas import tpu as pltpu
from jax.sharding import PartitionSpec as P

LEVELS = 32
LANES = 128
ROWS = 8
TOP = 8
MESH = pl.DeviceIdType.MESH
F32 = jnp.float32
BF16 = jnp.bfloat16


def sin_cos_small(angle):
    sq = angle * angle
    sin = angle + angle * sq * (-1.0 / 6 + sq * (1.0 / 120 + sq * (-1.0 / 5040 + sq * (1.0 / 362880))))
    cos = 1.0 + sq * (-0.5 + sq * (1.0 / 24 + sq * (-1.0 / 720 + sq * (1.0 / 40320 - sq * (1.0 / 3628800)))))
    return sin, cos


def kernel(
    size_x,
    size_y,
    size_s,
    width_y,
    now_hbm,
    before_hbm,
    forward_hbm,
    vel_hbm,
    eps_hbm,
    delta_hbm,
    tilt_hbm,
    azimuth_hbm,
    cell_hbm,
    count_ref,
    trace_hbm,
    next_hbm,
    gvel_hbm,
    geps_hbm,
    gdelta_hbm,
    field,
    before,
    forward,
    params,
    levels,
    own,
    cells,
    traces,
    parts,
    coef,
    surf,
    ha,
    sums,
    edge_out,
    edge_in,
    corner_in,
    far_in,
    near_in,
    result,
    grads,
    load_sem,
    out_sem,
    xs,
    xr,
    ys,
    yr,
    cs,
    cr,
    fs,
    fr,
    ns,
    nr,
):
    gx, gy, me = lax.axis_index("gx"), lax.axis_index("gy"), lax.axis_index("src")
    steps = 3
    nx = now_hbm.shape[2]
    ny = now_hbm.shape[3]
    nzb = now_hbm.shape[4] // LANES
    tiles = ny // ROWS
    body = pl.ds(TOP, ny)
    has_x = (gx > 0, gx < size_x - 1)
    has_y = (gy > 0, gy < size_y - 1)
    to_x = (gx - 1, gx + 1)
    to_y = (gy - 1, gy + 1)
    up = lax.rem(me + 1, size_s)
    down = lax.rem(me + size_s - 1, size_s)
    across = lax.rem(me + 2, size_s)

    def lanes_of(zb):
        return pl.ds(zb * LANES, LANES)

    loads = {}

    def load(name, index, src, dst):
        loads.setdefault(name, []).append(pltpu.make_async_copy(src, dst, load_sem.at[index]))

    for zb in range(nzb):
        load("now", zb, now_hbm.at[0, :, :, :, lanes_of(zb)], field.at[0, zb, :, pl.ds(1, nx), body, :])
    load("angle", nzb, tilt_hbm, levels.at[0])
    load("angle", nzb + 1, azimuth_hbm, levels.at[1])
    load("params", nzb + 2, vel_hbm, params.at[0])
    load("params", nzb + 3, eps_hbm, params.at[1])
    load("params", nzb + 4, delta_hbm, params.at[2])
    load("channels", nzb + 5, cell_hbm, cells)
    load("channels", nzb + 6, trace_hbm.at[0], traces)
    load("before", nzb + 7, before_hbm.at[0], before)
    load("forward", nzb + 8, forward_hbm.at[:, 0], forward)
    mine = pl.ds(pl.multiple_of(me * LANES, LANES), LANES)
    load("own", nzb + 9, vel_hbm.at[:, :, mine], own.at[0])
    load("own", nzb + 10, eps_hbm.at[:, :, mine], own.at[1])
    load("own", nzb + 11, delta_hbm.at[:, :, mine], own.at[2])
    for group in loads.values():
        for copy in group:
            copy.start()

    def arrived(name):
        for copy in loads[name]:
            copy.wait()

    barrier = pltpu.get_barrier_semaphore()
    greeted = jnp.int32(2)
    for dx in (0, 1):
        @pl.when(has_x[dx])
        def _():
            pl.semaphore_signal(barrier, inc=1, device_id={"gx": to_x[dx]}, device_id_type=MESH)
        greeted = greeted + has_x[dx].astype(jnp.int32)
    for dy in (0, 1):
        @pl.when(has_y[dy])
        def _():
            pl.semaphore_signal(barrier, inc=1, device_id={"gy": to_y[dy]}, device_id_type=MESH)
        greeted = greeted + has_y[dy].astype(jnp.int32)
    for dx in (0, 1):
        for dy in (0, 1):
            both = has_x[dx] & has_y[dy]
            @pl.when(both)
            def _():
                pl.semaphore_signal(
                    barrier, inc=1, device_id={"gx": to_x[dx], "gy": to_y[dy]}, device_id_type=MESH
                )
            greeted = greeted + both.astype(jnp.int32)
    for peer in (up, down):
        pl.semaphore_signal(barrier, inc=1, device_id={"src": peer}, device_id_type=MESH)

    for dx in (0, 1):
        @pl.when(jnp.logical_not(has_x[dx]))
        def _():
            plane = (0, nx + 1)[dx]
            zeros = jnp.zeros((ny + 2 * TOP, LANES), F32)
            @pl.loop(0, steps)
            def _(t):
                for zb in range(nzb):
                    for c in (0, 1):
                        field[t, zb, c, plane] = zeros
    for dy in (0, 1):
        @pl.when(jnp.logical_not(has_y[dy]))
        def _():
            row = (TOP - 1, TOP + ny)[dy]
            zeros = jnp.zeros((1, LANES), F32)
            @pl.loop(0, steps)
            def _(t):
                for zb in range(nzb):
                    for c in (0, 1):
                        for x in range(nx + 2):
                            field[t, zb, c, x, pl.ds(row, 1)] = zeros
    pl.semaphore_wait(barrier, greeted)

    def face(t, dx):
        return pltpu.make_async_remote_copy(
            src_ref=field.at[t, :, :, (1, nx)[dx], body, :],
            dst_ref=field.at[t, :, :, (nx + 1, 0)[dx], body, :],
            send_sem=xs.at[t, dx],
            recv_sem=xr.at[t, dx],
            device_id={"gx": to_x[dx]},
            device_id_type=MESH,
        )

    def first_face(zb, dx):
        return pltpu.make_async_remote_copy(
            src_ref=now_hbm.at[0, :, (0, nx - 1)[dx], :, lanes_of(zb)],
            dst_ref=field.at[0, zb, :, (nx + 1, 0)[dx], body, :],
            send_sem=xs.at[0, dx],
            recv_sem=xr.at[0, dx],
            device_id={"gx": to_x[dx]},
            device_id_type=MESH,
        )

    def edge(t, dy):
        return pltpu.make_async_remote_copy(
            src_ref=edge_out.at[t, dy],
            dst_ref=edge_in.at[t, dy],
            send_sem=ys.at[t, dy],
            recv_sem=yr.at[t, dy],
            device_id={"gy": to_y[dy]},
            device_id_type=MESH,
        )

    def corner(t, dx, dy):
        return pltpu.make_async_remote_copy(
            src_ref=edge_out.at[t, dy, (0, nx - 1)[dx]],
            dst_ref=corner_in.at[t, dx, dy],
            send_sem=cs.at[t, dx, dy],
            recv_sem=cr.at[t, dx, dy],
            device_id={"gx": to_x[dx], "gy": to_y[dy]},
            device_id_type=MESH,
        )

    def send_faces(t):
        for dx in (0, 1):
            @pl.when(has_x[dx])
            def _():
                face(t, dx).start()

    def send_edges(t):
        for x in range(nx):
            for zb in range(nzb):
                for c in (0, 1):
                    slot = pl.ds(zb * 2 + c, 1)
                    edge_out[t, 0, x, slot] = field[t, zb, c, x + 1, pl.ds(TOP, 1)]
                    edge_out[t, 1, x, slot] = field[t, zb, c, x + 1, pl.ds(TOP + ny - 1, 1)]
        for dy in (0, 1):
            @pl.when(has_y[dy])
            def _():
                edge(t, dy).start()
        for dx in (0, 1):
            for dy in (0, 1):
                @pl.when(has_x[dx] & has_y[dy])
                def _():
                    corner(t, dx, dy).start()

    def receive_edges(t):
        for dy in (0, 1):
            @pl.when(has_y[1 - dy])
            def _():
                edge(t, dy).wait_recv()
                row = (TOP + ny, TOP - 1)[dy]
                for x in range(nx):
                    for zb in range(nzb):
                        for c in (0, 1):
                            field[t, zb, c, x + 1, pl.ds(row, 1)] = edge_in[t, dy, x, pl.ds(zb * 2 + c, 1)]

    def receive_faces(t):
        for dx in (0, 1):
            for dy in (0, 1):
                @pl.when(has_x[1 - dx] & has_y[1 - dy])
                def _():
                    corner(t, dx, dy).wait_recv()
                    row = (TOP + ny, TOP - 1)[dy]
                    for zb in range(nzb):
                        for c in (0, 1):
                            field[t, zb, c, (nx + 1, 0)[dx], pl.ds(row, 1)] = corner_in[
                                t, dx, dy, pl.ds(zb * 2 + c, 1)
                            ]
        for dx in (0, 1):
            @pl.when(has_x[1 - dx])
            def _():
                face(t, dx).wait_recv()

    for dx in (0, 1):
        @pl.when(has_x[dx])
        def _():
            for zb in range(nzb):
                first_face(zb, dx).start()
    arrived("now")
    send_edges(0)

    arrived("angle")
    arrived("params")

    @pl.loop(0, nx)
    def _(x):
        for tile in range(tiles):
            rows = pl.ds(tile * ROWS, ROWS)
            for zb in range(nzb):
                cols = lanes_of(zb)
                tilt = levels[0, x, rows, cols].astype(F32)
                turn = levels[1, x, rows, cols].astype(F32)
                sin_h, cos_h = sin_cos_small(tilt * (0.5 * math.pi / LEVELS) - 0.25 * math.pi)
                sin_t = (sin_h + cos_h) * math.sqrt(0.5)
                cos_t = (cos_h - sin_h) * math.sqrt(0.5)
                sin_q, cos_q = sin_cos_small(turn * (0.5 * math.pi / LEVELS) - 0.25 * math.pi)
                sin_2, cos_2 = 2.0 * sin_q * cos_q, 1.0 - 2.0 * sin_q * sin_q
                sin_p, cos_p = -2.0 * sin_2 * cos_2, 2.0 * sin_2 * sin_2 - 1.0
                flat = sin_t * sin_t
                slope = 0.5 * sin_t * cos_t
                coef[0, x, zb, rows] = flat * cos_p * cos_p
                coef[1, x, zb, rows] = flat * sin_p * sin_p
                coef[2, x, zb, rows] = cos_t * cos_t
                coef[3, x, zb, rows] = 0.5 * flat * sin_p * cos_p
                coef[4, x, zb, rows] = slope * sin_p
                coef[5, x, zb, rows] = slope * cos_p
                vel = params[0, x, rows, cols]
                coef[6, x, zb, rows] = vel * vel
                coef[7, x, zb, rows] = 1.0 + 2.0 * params[1, x, rows, cols]
                coef[8, x, zb, rows] = jnp.sqrt(1.0 + 2.0 * params[2, x, rows, cols])

    arrived("channels")
    cell = cells[...]
    local_x = cell // width_y - gx * nx
    local_y = cell % width_y - gy * ny
    slots = lax.broadcasted_iota(jnp.int32, cell.shape, 1)
    inside = (local_x >= 0) & (local_x < nx) & (local_y >= 0) & (local_y < ny) & (slots < count_ref[0])
    target = jnp.where(inside, local_x * ny + local_y, -1)
    spots = lax.broadcasted_iota(jnp.int32, (nx * ny, cell.shape[1]), 0)
    onehot = jnp.where(target == spots, 1.0, 0.0).astype(BF16)
    value = traces[...]
    high = value.astype(BF16).astype(F32)
    middle = (value - high).astype(BF16).astype(F32)
    low = (value - high) - middle
    parts[...] = jnp.zeros_like(parts)
    parts[pl.ds(0, steps)] = high
    parts[pl.ds(steps, steps)] = middle
    parts[pl.ds(2 * steps, steps)] = low
    table = lax.dot_general(
        onehot, parts[...].astype(BF16), (((1,), (1,)), ((), ())), preferred_element_type=F32
    )
    table = table + pltpu.roll(table, LANES - steps, 1) + pltpu.roll(table, LANES - 2 * steps, 1)
    spot_lane = lax.broadcasted_iota(jnp.int32, table.shape, 1)
    for t in range(steps):
        moved = table if t == 0 else pltpu.roll(table, LANES - t, 1)
        surf[t] = jnp.where(spot_lane == 0, moved, 0.0)

    lane = lax.broadcasted_iota(jnp.int32, (ROWS, LANES), 1)
    first, last = lane == 0, lane == LANES - 1
    zero = jnp.zeros((ROWS, LANES), F32)

    def shifted(blocks):
        ahead = [pltpu.roll(block, LANES - 1, 1) for block in blocks] + [zero]
        behind = [zero] + [pltpu.roll(block, 1, 1) for block in blocks]
        after = [jnp.where(last, ahead[i + 1], ahead[i]) for i in range(nzb)]
        prior = [jnp.where(first, behind[i], behind[i + 1]) for i in range(nzb)]
        return after, prior

    def stencil(t, c, x, tile, weights):
        def read(dx, dy):
            rows = pl.ds(TOP + tile * ROWS + dy, ROWS)
            return [field[t, zb, c, x + 1 + dx, rows] for zb in range(nzb)]

        center, right, left, north, south = read(0, 0), read(1, 0), read(-1, 0), read(0, 1), read(0, -1)
        slope_y = [a - b for a, b in zip(north, south)]
        slope_x = [a - b for a, b in zip(right, left)]
        cross = [(a - b) - (d - e) for a, b, d, e in zip(read(1, 1), read(1, -1), read(-1, 1), read(-1, -1))]
        after, prior = shifted(center)
        after_y, prior_y = shifted(slope_y)
        after_x, prior_x = shifted(slope_x)
        out = []
        for zb in range(nzb):
            w = weights[zb]
            sum_x = right[zb] + left[zb]
            sum_y = north[zb] + south[zb]
            sum_z = after[zb] + prior[zb]
            mixed = (
                w[0] * sum_x
                + w[1] * sum_y
                + w[2] * sum_z
                + w[3] * cross[zb]
                + w[4] * (after_y[zb] - prior_y[zb])
                + w[5] * (after_x[zb] - prior_x[zb])
            )
            twice = center[zb] + center[zb]
            if c == 0:
                out.append((sum_x + sum_y + sum_z) - (twice + twice) - mixed)
            else:
                out.append(mixed - twice)
        return out

    def advance(t, x, tile):
        rows = pl.ds(tile * ROWS, ROWS)
        for zb in range(nzb):
            cols = lanes_of(zb)
            horiz, axial = ha[0, x, zb, rows], ha[1, x, zb, rows]
            speed, stretch, root = (coef[i, x, zb, rows] for i in (6, 7, 8))
            updates = (stretch * horiz + root * axial, root * horiz + axial)
            for c in (0, 1):
                here = pl.ds(TOP + tile * ROWS, ROWS)
                center = field[t, zb, c, x + 1, here]
                old = before[c, x, rows, cols] if t == 0 else field[t - 1, zb, c, x + 1, here]
                following = (center + center) - old + speed * updates[c]
                if zb == 0 and c == 0:
                    start = pl.multiple_of(x * ny + tile * ROWS, ROWS)
                    following = following + surf[t, pl.ds(start, ROWS)]
                if t == steps - 1:
                    result[c, x, rows, cols] = following
                else:
                    field[t + 1, zb, c, x + 1, here] = following

    def operators(t, x):
        for tile in range(tiles):
            rows = pl.ds(tile * ROWS, ROWS)
            weights = [[coef[i, x, zb, rows] for i in range(6)] for zb in range(nzb)]
            for c in (0, 1):
                out = stencil(t, c, x, tile, weights)
                for zb in range(nzb):
                    ha[c, x, zb, rows] = out[zb]
            if t < steps - 1:
                advance(t, x, tile)

    def accumulate(t, x):
        for half in range(ny // 16):
            rows = pl.ds(half * 16, 16)
            for zb in range(nzb):
                cols = lanes_of(zb)
                horiz, axial = ha[0, x, zb, rows], ha[1, x, zb, rows]
                pf = forward[t, 0, x, rows, cols].astype(F32)
                qf = forward[t, 1, x, rows, cols].astype(F32)
                terms = (pf * horiz, pf * axial + qf * horiz, qf * axial)
                for i in range(3):
                    sums[zb, i, x, rows] = terms[i] if t == 0 else sums[zb, i, x, rows] + terms[i]

    half = nx // 2
    inner, outer = list(range(1, nx - 1)), [0, nx - 1]

    def far(x):
        way = 0 if x < half else 1
        return pltpu.make_async_remote_copy(
            src_ref=sums.at[across, :, x],
            dst_ref=far_in.at[x],
            send_sem=fs.at[x],
            recv_sem=fr.at[x],
            device_id={"src": (up, down)[way]},
            device_id_type=MESH,
        )

    def near(x, way):
        return pltpu.make_async_remote_copy(
            src_ref=sums.at[(up, down)[way], :, x],
            dst_ref=near_in.at[way, x],
            send_sem=ns.at[way, x],
            recv_sem=nr.at[way, x],
            device_id={"src": (up, down)[way]},
            device_id_type=MESH,
        )

    arrived("before")
    for t in range(steps):
        final = t == steps - 1

        def plane(x):
            operators(t, x)
            if final:
                accumulate(t, x)

        receive_edges(t)

        @pl.loop(1, nx - 1)
        def _(x):
            plane(x)

        if final:
            for x in inner:
                far(x).start()
            for x in inner:
                near(x, 1 if x < half else 0).start()
        receive_faces(t)
        if not final:
            @pl.loop(0, 2)
            def _(i):
                plane(i * (nx - 1))

            send_faces(t + 1)
            send_edges(t + 1)
            if t == 0:
                arrived("forward")

            @pl.loop(0, nx)
            def _(x):
                accumulate(t, x)
        else:
            @pl.loop(0, 2)
            def _(i):
                plane(i * (nx - 1))

    for x in outer:
        far(x).start()
    for x in outer:
        near(x, 1 if x < half else 0).start()

    @pl.loop(0, nx)
    def _(x):
        for tile in range(tiles):
            advance(steps - 1, x, tile)

    out_copy = pltpu.make_async_copy(result, next_hbm.at[0], out_sem.at[0])
    out_copy.start()
    for x in inner + outer:
        way = 0 if x < half else 1
        far(x).wait_recv()
        for i in range(3):
            sums[(up, down)[way], i, x] = sums[(up, down)[way], i, x] + far_in[x, i]
        near(x, way).start()

    arrived("own")
    for x in inner + outer:
        for way in (0, 1):
            near(x, way).wait_recv()
        for tile in range(tiles):
            rows = pl.ds(tile * ROWS, ROWS)
            a, b, c = (
                sums[me, i, x, rows] + near_in[0, x, i, rows] + near_in[1, x, i, rows] for i in range(3)
            )
            vel = own[0, x, rows]
            stretch = 1.0 + 2.0 * own[1, x, rows]
            root = jnp.sqrt(1.0 + 2.0 * own[2, x, rows])
            speed = vel * vel
            grads[0, x, rows] = 2.0 * vel * (stretch * a + root * b + c)
            grads[1, x, rows] = 2.0 * speed * a
            grads[2, x, rows] = speed / root * b
    grad_copies = [
        pltpu.make_async_copy(grads.at[i], out, out_sem.at[1 + i])
        for i, out in enumerate((gvel_hbm, geps_hbm, gdelta_hbm))
    ]
    for copy in grad_copies:
        copy.start()

    for t in range(steps):
        for dx in (0, 1):
            @pl.when(has_x[dx])
            def _():
                face(t, dx).wait_send()
        for dy in (0, 1):
            @pl.when(has_y[dy])
            def _():
                edge(t, dy).wait_send()
        for dx in (0, 1):
            for dy in (0, 1):
                @pl.when(has_x[dx] & has_y[dy])
                def _():
                    corner(t, dx, dy).wait_send()
    for x in range(nx):
        far(x).wait_send()
        for way in (0, 1):
            near(x, way).wait_send()
    out_copy.wait()
    for copy in grad_copies:
        copy.wait()


def on_device(
    adjoint_now,
    adjoint_before,
    forward_field,
    velocity,
    thomsen_eps,
    thomsen_delta,
    tilt_level,
    azimuth_level,
    channel_cell,
    channel_count,
    residual_trace,
):
    nx, ny, depth = velocity.shape
    nzb = depth // LANES
    steps = forward_field.shape[0]
    channels = channel_cell.shape[1]
    size_x, size_y, size_s = (lax.axis_size(name) for name in ("gx", "gy", "src"))
    block = jax.ShapeDtypeStruct((nx, ny, LANES), F32)
    anywhere = pl.BlockSpec(memory_space=pl.ANY)
    dma = pltpu.SemaphoreType.DMA
    return pl.pallas_call(
        functools.partial(kernel, size_x, size_y, size_s, ny * size_y),
        name="adjoint_steps",
        out_shape=(jax.ShapeDtypeStruct(adjoint_now.shape, F32), block, block, block),
        in_specs=[anywhere] * 9 + [pl.BlockSpec(memory_space=pltpu.SMEM), anywhere],
        out_specs=(anywhere,) * 4,
        scratch_shapes=[
            pltpu.VMEM((steps, nzb, 2, nx + 2, ny + 2 * TOP, LANES), F32),
            pltpu.VMEM((2, nx, ny, depth), F32),
            pltpu.VMEM((steps, 2, nx, ny, depth), BF16),
            pltpu.VMEM((3, nx, ny, depth), F32),
            pltpu.VMEM((2, nx, ny, depth), jnp.int32),
            pltpu.VMEM((3, nx, ny, LANES), F32),
            pltpu.VMEM((1, channels), jnp.int32),
            pltpu.VMEM((steps, channels), F32),
            pltpu.VMEM((LANES, channels), F32),
            pltpu.VMEM((9, nx, nzb, ny, LANES), F32),
            pltpu.VMEM((steps, nx * ny, LANES), F32),
            pltpu.VMEM((2, nx, nzb, ny, LANES), F32),
            pltpu.VMEM((nzb, 3, nx, ny, LANES), F32),
            pltpu.VMEM((steps, 2, nx, 2 * nzb, LANES), F32),
            pltpu.VMEM((steps, 2, nx, 2 * nzb, LANES), F32),
            pltpu.VMEM((steps, 2, 2, 2 * nzb, LANES), F32),
            pltpu.VMEM((nx, 3, ny, LANES), F32),
            pltpu.VMEM((2, nx, 3, ny, LANES), F32),
            pltpu.VMEM((2, nx, ny, depth), F32),
            pltpu.VMEM((3, nx, ny, LANES), F32),
            dma((nzb + 12,)),
            dma((4,)),
            dma((steps, 2)),
            dma((steps, 2)),
            dma((steps, 2)),
            dma((steps, 2)),
            dma((steps, 2, 2)),
            dma((steps, 2, 2)),
            dma((nx,)),
            dma((nx,)),
            dma((2, nx)),
            dma((2, nx)),
        ],
        compiler_params=pltpu.CompilerParams(
            collective_id=0, has_side_effects=True, vmem_limit_bytes=48 * 1024 * 1024
        ),
    )(
        adjoint_now,
        adjoint_before,
        forward_field,
        velocity,
        thomsen_eps,
        thomsen_delta,
        tilt_level,
        azimuth_level,
        channel_cell,
        channel_count,
        residual_trace,
    )


def solution(mesh):
    placed = (
        P("src", None, "gx", "gy", None),
        P("src", None, "gx", "gy", None),
        P(None, "src", None, "gx", "gy", None),
        P("gx", "gy", None),
        P("gx", "gy", None),
        P("gx", "gy", None),
        P("gx", "gy", None),
        P("gx", "gy", None),
        P("src", None),
        P("src"),
        P("src", None, None),
    )
    return jax.shard_map(
        on_device,
        mesh=mesh,
        in_specs=placed,
        out_specs=(
            P("src", None, "gx", "gy", None),
            P("gx", "gy", "src"),
            P("gx", "gy", "src"),
            P("gx", "gy", "src"),
        ),
        check_vma=False,
    )
```

time: 239 us -> 53.2 us (0.22); the launches traced: 236 us -> 52.8 us
  waiting for transfers between devices: 148 us -> 0 us
  Pallas kernels: 0 us -> 40.1 us
  starting transfers between devices: 35.4 us -> 0 us
  other arithmetic: 16 us -> 0 us
  between operations: 16.1 us -> 1.31 us
  local copies, waits for them, and re-layouts: 20.6 us -> 11.4 us
    unnamed x2 -> x0, waiting for transfers between devices: 132 us -> none
    pallas_call x0 -> x1, Pallas kernels: none -> 40.1 us  [on_device(): pl.pallas_call(functools.partial(kernel, size_x, size_y, size_s, ny * siz...]
    ppermute x12 -> x0, starting transfers between devices: 35.4 us -> none  [the longest x6 21 us: extended_2(): lax.ppermute(lax.slice_in_dim(block, block.shape[dim] - width, None, axis...]
    ppermute x12 -> x0, waiting for transfers between devices: 15.1 us -> none  [the longest x6 14.4 us: extended_2(): lax.ppermute(lax.slice_in_dim(block, block.shape[dim] - width, None, axis...]
    add x14 -> x0, other arithmetic: 10.1 us -> none  [the longest x3 5.88 us: split_operators(): axial = axial + weights[index] * parts[index]]
    add x3 -> x0, local copies, waits for them, and re-layouts: 5.07 us -> none  [the longest x1 2.38 us: on_device(): total_epsilon = total_epsilon + term_epsilon]
    mul x2 -> x0, other arithmetic: 3.41 us -> none  [the longest x1 3.37 us: tilt_weights(): sin_t * sin_t * cos_p * cos_p]
    unnamed x92 -> x23, local copies, waits for them, and re-layouts: 10 us -> 11.4 us
  transfers between devices with their start and end apart: 13 -> 0, of which waited for: 7 -> 0; matrix products, arithmetic and copies ran while one was open for 4% -> 0% of each run, Pallas kernels for 0% -> 0%
where the time goes in v1:
time: 53.2 us; the launch traced here: 52.8 us
  Pallas kernels  40.1 us (75%)
  local copies, waits for them, and re-layouts  11.4 us (21%)
  between operations  1.31 us (2%)
    pallas_call x1, Pallas kernels, on_device(): pl.pallas_call(functools.partial(kernel, size_x, size_y, size_s, ny * siz...  40.1 us
    unnamed x23, local copies, waits for them, and re-layouts  11.4 us

profile of v1, /device:TPU:32, one launch (start us, length us, event | category | flops | bytes accessed | tf_op | source)
XLA Modules:
  0.0 52.8 jit_solution(6263448430289281958)
XLA Ops:
  1.3 0.0 copy-start.8
  1.3 0.7 %copy.15.trace_hbm = f32[1,3,1536]{2,1,0:T(4,128)S(1)} copy(f32[1,3,1536]{2,0,1:T(1,128)} %param.21) | data formatting | bytes 36864 | tf_op args[10]
  2.0 0.0 copy-done.8
  2.0 0.0 copy-start
  2.0 1.1 %copy-done = bf16[3,1,2,4,32,512]{5,4,3,2,1,0:T(8,128)(2,1)S(1)} copy-done((bf16[3,1,2,4,32,512]{5,4,3,2,1,0:T(8,128)(2,1)S(1)}, bf16[3,1,2,4,32,512]{5,4,3,2,1,0:T(8,128)(2,1)}, u32[]{:S(2)}) %copy-start) | copy-done | bytes 786456
  3.2 0.0 copy-start.1
  3.2 1.0 %copy-done.1 = f32[1,2,4,32,512]{4,3,2,1,0:T(8,128)S(1)} copy-done((f32[1,2,4,32,512]{4,3,2,1,0:T(8,128)S(1)}, f32[1,2,4,32,512]{4,3,2,1,0:T(8,128)}, u32[]{:S(2)}) %copy-start.1) | copy-done | bytes 524312
  4.2 0.0 copy-start.2
  4.2 1.0 %copy-done.2 = f32[1,2,4,32,512]{4,3,2,1,0:T(8,128)S(1)} copy-done((f32[1,2,4,32,512]{4,3,2,1,0:T(8,128)S(1)}, f32[1,2,4,32,512]{4,3,2,1,0:T(8,128)}, u32[]{:S(2)}) %copy-start.2) | copy-done | bytes 524312
  5.2 0.0 copy-start.3
  5.3 0.9 %copy-done.3 = f32[4,32,512]{2,1,0:T(8,128)S(1)} copy-done((f32[4,32,512]{2,1,0:T(8,128)S(1)}, f32[4,32,512]{2,1,0:T(8,128)}, u32[]{:S(2)}) %copy-start.3) | copy-done | bytes 262168
  6.2 0.0 copy-start.4
  6.2 0.9 %copy-done.4 = f32[4,32,512]{2,1,0:T(8,128)S(1)} copy-done((f32[4,32,512]{2,1,0:T(8,128)S(1)}, f32[4,32,512]{2,1,0:T(8,128)}, u32[]{:S(2)}) %copy-start.4) | copy-done | bytes 262168
  7.2 0.0 copy-start.5
  7.2 0.9 %copy-done.5 = f32[4,32,512]{2,1,0:T(8,128)S(1)} copy-done((f32[4,32,512]{2,1,0:T(8,128)S(1)}, f32[4,32,512]{2,1,0:T(8,128)}, u32[]{:S(2)}) %copy-start.5) | copy-done | bytes 262168
  8.1 0.0 copy-start.6
  8.1 0.9 %copy-done.6 = s32[4,32,512]{2,1,0:T(8,128)S(1)} copy-done((s32[4,32,512]{2,1,0:T(8,128)S(1)}, s32[4,32,512]{2,1,0:T(8,128)}, u32[]{:S(2)}) %copy-start.6) | copy-done | bytes 262168
  9.1 0.0 copy-start.7
  9.1 0.9 %copy-done.7 = s32[4,32,512]{2,1,0:T(8,128)S(1)} copy-done((s32[4,32,512]{2,1,0:T(8,128)S(1)}, s32[4,32,512]{2,1,0:T(8,128)}, u32[]{:S(2)}) %copy-start.7) | copy-done | bytes 262168
  10.0 40.1 %adjoint_steps.1 = (f32[1,2,4,32,512]{4,3,2,1,0:T(8,128)S(1)}, f32[4,32,128]{2,1,0:T(8,128)S(1)}, f32[4,32,128]{2,1,0:T(8,128)S(1)}, f32[4,32,128]{2,1,0:T(8,128)S(1)}) custom-call(f32[1,2,4,32,512]{4,3,2,1,0:T(8,128)S(1)} %copy-done.1, f32[1,2,4,32,512]{4,3,2,1,0:T(8,128)S(1)} %copy-done.2, bf16[3,1,2,4,32,512]{5,4,3,2,1,0:T(8,128)(2,1)S(1)} %copy-done, ...), custom_call_target="tpu_custom_call" | custom-call | tf_op jit(solution)/shard_map/adjoint_steps/pallas_call | solution.py:564
  50.1 0.8 %copy.21 = f32[1,2,4,32,512]{4,3,2,1,0:T(8,128)} copy(f32[1,2,4,32,512]{4,3,2,1,0:T(8,128)S(1)} %get-tuple-element.8) | data formatting | bytes 1048576
  50.9 0.6 %copy.22 = f32[4,32,128]{2,1,0:T(8,128)} copy(f32[4,32,128]{2,1,0:T(8,128)S(1)} %get-tuple-element.9) | data formatting | bytes 131072
  51.5 0.6 %copy.23 = f32[4,32,128]{2,1,0:T(8,128)} copy(f32[4,32,128]{2,1,0:T(8,128)S(1)} %get-tuple-element.10) | data formatting | bytes 131072
  52.1 0.6 %copy.24 = f32[4,32,128]{2,1,0:T(8,128)} copy(f32[4,32,128]{2,1,0:T(8,128)S(1)} %get-tuple-element.11) | data formatting | bytes 131072
Async XLA Ops:
  1.3 0.7 %copy-start.8 = (s32[1,1536]{1,0:T(1,128)S(1)}, s32[1,1536]{1,0:T(1,128)}, u32[]{:S(2)}) copy-start(s32[1,1536]{1,0:T(1,128)} %cell_hbm.1) | copy-start | bytes 18436
  2.0 1.1 %copy-start = (bf16[3,1,2,4,32,512]{5,4,3,2,1,0:T(8,128)(2,1)S(1)}, bf16[3,1,2,4,32,512]{5,4,3,2,1,0:T(8,128)(2,1)}, u32[]{:S(2)}) copy-start(bf16[3,1,2,4,32,512]{5,4,3,2,1,0:T(8,128)(2,1)} %forward_hbm.1) | copy-start | bytes 2359300
  3.2 1.0 %copy-start.1 = (f32[1,2,4,32,512]{4,3,2,1,0:T(8,128)S(1)}, f32[1,2,4,32,512]{4,3,2,1,0:T(8,128)}, u32[]{:S(2)}) copy-start(f32[1,2,4,32,512]{4,3,2,1,0:T(8,128)} %now_hbm.1) | copy-start | bytes 1572868
  4.2 1.0 %copy-start.2 = (f32[1,2,4,32,512]{4,3,2,1,0:T(8,128)S(1)}, f32[1,2,4,32,512]{4,3,2,1,0:T(8,128)}, u32[]{:S(2)}) copy-start(f32[1,2,4,32,512]{4,3,2,1,0:T(8,128)} %before_hbm.1) | copy-start | bytes 1572868
  5.2 0.9 %copy-start.3 = (f32[4,32,512]{2,1,0:T(8,128)S(1)}, f32[4,32,512]{2,1,0:T(8,128)}, u32[]{:S(2)}) copy-start(f32[4,32,512]{2,1,0:T(8,128)} %vel_hbm.1) | copy-start | bytes 786436
  6.2 0.9 %copy-start.4 = (f32[4,32,512]{2,1,0:T(8,128)S(1)}, f32[4,32,512]{2,1,0:T(8,128)}, u32[]{:S(2)}) copy-start(f32[4,32,512]{2,1,0:T(8,128)} %eps_hbm.1) | copy-start | bytes 786436
  7.2 0.9 %copy-start.5 = (f32[4,32,512]{2,1,0:T(8,128)S(1)}, f32[4,32,512]{2,1,0:T(8,128)}, u32[]{:S(2)}) copy-start(f32[4,32,512]{2,1,0:T(8,128)} %delta_hbm.1) | copy-start | bytes 786436
  8.1 0.9 %copy-start.6 = (s32[4,32,512]{2,1,0:T(8,128)S(1)}, s32[4,32,512]{2,1,0:T(8,128)}, u32[]{:S(2)}) copy-start(s32[4,32,512]{2,1,0:T(8,128)} %tilt_hbm.1) | copy-start | bytes 786436
  9.1 0.9 %copy-start.7 = (s32[4,32,512]{2,1,0:T(8,128)S(1)}, s32[4,32,512]{2,1,0:T(8,128)}, u32[]{:S(2)}) copy-start(s32[4,32,512]{2,1,0:T(8,128)} %azimuth_hbm.1) | copy-start | bytes 786436

commit v2 on v1

--- a/solution.py
+++ b/solution.py
@@ -13,6 +13,7 @@
 ROWS = 8
 TOP = 8
 MESH = pl.DeviceIdType.MESH
+CROSS, CHIP = 0, 1
 F32 = jnp.float32
 BF16 = jnp.bfloat16
 
@@ -84,9 +85,16 @@
     nzb = now_hbm.shape[4] // LANES
     tiles = ny // ROWS
     body = pl.ds(TOP, ny)
-    has_x = (gx > 0, gx < size_x - 1)
+    even = lax.rem(gx, 2) == 0
+    below, above = gx > 0, gx < size_x - 1
+    has_x = (even & below | ~even & above, even & above | ~even & below)
+    sign = jnp.where(even, 1, -1)
+    to_x = (gx - sign, gx + sign)
+    rim = (jnp.where(even, 0, nx - 1), jnp.where(even, nx - 1, 0))
+    halo = (jnp.where(even, 0, nx + 1), jnp.where(even, nx + 1, 0))
+    landing = (halo[1], halo[0])
+    early = jnp.where(even, 1, 0)
     has_y = (gy > 0, gy < size_y - 1)
-    to_x = (gx - 1, gx + 1)
     to_y = (gy - 1, gy + 1)
     up = lax.rem(me + 1, size_s)
     down = lax.rem(me + size_s - 1, size_s)
@@ -108,7 +116,7 @@
     load("params", nzb + 3, eps_hbm, params.at[1])
     load("params", nzb + 4, delta_hbm, params.at[2])
     load("channels", nzb + 5, cell_hbm, cells)
-    load("channels", nzb + 6, trace_hbm.at[0], traces)
+    load("channels", nzb + 6, trace_hbm.at[:, 0], traces)
     load("before", nzb + 7, before_hbm.at[0], before)
     load("forward", nzb + 8, forward_hbm.at[:, 0], forward)
     mine = pl.ds(pl.multiple_of(me * LANES, LANES), LANES)
@@ -125,38 +133,37 @@
 
     barrier = pltpu.get_barrier_semaphore()
     greeted = jnp.int32(2)
-    for dx in (0, 1):
-        @pl.when(has_x[dx])
+    for side in (CROSS, CHIP):
+        @pl.when(has_x[side])
         def _():
-            pl.semaphore_signal(barrier, inc=1, device_id={"gx": to_x[dx]}, device_id_type=MESH)
-        greeted = greeted + has_x[dx].astype(jnp.int32)
+            pl.semaphore_signal(barrier, inc=1, device_id={"gx": to_x[side]}, device_id_type=MESH)
+        greeted = greeted + has_x[side].astype(jnp.int32)
     for dy in (0, 1):
         @pl.when(has_y[dy])
         def _():
             pl.semaphore_signal(barrier, inc=1, device_id={"gy": to_y[dy]}, device_id_type=MESH)
         greeted = greeted + has_y[dy].astype(jnp.int32)
-    for dx in (0, 1):
+    for side in (CROSS, CHIP):
         for dy in (0, 1):
-            both = has_x[dx] & has_y[dy]
+            both = has_x[side] & has_y[dy]
             @pl.when(both)
             def _():
                 pl.semaphore_signal(
-                    barrier, inc=1, device_id={"gx": to_x[dx], "gy": to_y[dy]}, device_id_type=MESH
+                    barrier, inc=1, device_id={"gx": to_x[side], "gy": to_y[dy]}, device_id_type=MESH
                 )
             greeted = greeted + both.astype(jnp.int32)
     for peer in (up, down):
         pl.semaphore_signal(barrier, inc=1, device_id={"src": peer}, device_id_type=MESH)
 
-    for dx in (0, 1):
-        @pl.when(jnp.logical_not(has_x[dx]))
+    for side in (CROSS, CHIP):
+        @pl.when(jnp.logical_not(has_x[side]))
         def _():
-            plane = (0, nx + 1)[dx]
             zeros = jnp.zeros((ny + 2 * TOP, LANES), F32)
             @pl.loop(0, steps)
             def _(t):
                 for zb in range(nzb):
                     for c in (0, 1):
-                        field[t, zb, c, plane] = zeros
+                        field[t, zb, c, halo[side]] = zeros
     for dy in (0, 1):
         @pl.when(jnp.logical_not(has_y[dy]))
         def _():
@@ -168,106 +175,110 @@
                     for c in (0, 1):
                         for x in range(nx + 2):
                             field[t, zb, c, x, pl.ds(row, 1)] = zeros
-    pl.semaphore_wait(barrier, greeted)
-
-    def face(t, dx):
+
+    def face(t, side):
         return pltpu.make_async_remote_copy(
-            src_ref=field.at[t, :, :, (1, nx)[dx], body, :],
-            dst_ref=field.at[t, :, :, (nx + 1, 0)[dx], body, :],
-            send_sem=xs.at[t, dx],
-            recv_sem=xr.at[t, dx],
-            device_id={"gx": to_x[dx]},
+            src_ref=field.at[t, :, :, rim[side] + 1, body, :],
+            dst_ref=field.at[t, :, :, landing[side], body, :],
+            send_sem=xs.at[t, side],
+            recv_sem=xr.at[t, side],
+            device_id={"gx": to_x[side]},
             device_id_type=MESH,
         )
 
-    def first_face(zb, dx):
+    def first_face(zb, side):
         return pltpu.make_async_remote_copy(
-            src_ref=now_hbm.at[0, :, (0, nx - 1)[dx], :, lanes_of(zb)],
-            dst_ref=field.at[0, zb, :, (nx + 1, 0)[dx], body, :],
-            send_sem=xs.at[0, dx],
-            recv_sem=xr.at[0, dx],
-            device_id={"gx": to_x[dx]},
+            src_ref=now_hbm.at[0, :, rim[side], :, lanes_of(zb)],
+            dst_ref=field.at[0, zb, :, landing[side], body, :],
+            send_sem=xs.at[0, side],
+            recv_sem=xr.at[0, side],
+            device_id={"gx": to_x[side]},
             device_id_type=MESH,
         )
 
-    def edge(t, dy):
+    def planes_of(group):
+        return pl.ds(rim[CROSS], 1) if group == CROSS else pl.ds(early, nx - 1)
+
+    def edge(t, dy, group):
         return pltpu.make_async_remote_copy(
-            src_ref=edge_out.at[t, dy],
-            dst_ref=edge_in.at[t, dy],
-            send_sem=ys.at[t, dy],
-            recv_sem=yr.at[t, dy],
+            src_ref=edge_out.at[t, dy, planes_of(group)],
+            dst_ref=edge_in.at[t, dy, planes_of(group)],
+            send_sem=ys.at[t, dy, group],
+            recv_sem=yr.at[t, dy, group],
             device_id={"gy": to_y[dy]},
             device_id_type=MESH,
         )
 
-    def corner(t, dx, dy):
+    def corner(t, side, dy):
         return pltpu.make_async_remote_copy(
-            src_ref=edge_out.at[t, dy, (0, nx - 1)[dx]],
-            dst_ref=corner_in.at[t, dx, dy],
-            send_sem=cs.at[t, dx, dy],
-            recv_sem=cr.at[t, dx, dy],
-            device_id={"gx": to_x[dx], "gy": to_y[dy]},
+            src_ref=edge_out.at[t, dy, rim[side]],
+            dst_ref=corner_in.at[t, side, dy],
+            send_sem=cs.at[t, side, dy],
+            recv_sem=cr.at[t, side, dy],
+            device_id={"gx": to_x[side], "gy": to_y[dy]},
             device_id_type=MESH,
         )
 
-    def send_faces(t):
-        for dx in (0, 1):
-            @pl.when(has_x[dx])
-            def _():
-                face(t, dx).start()
-
-    def send_edges(t):
-        for x in range(nx):
+    def send_face(t, side):
+        @pl.when(has_x[side])
+        def _():
+            face(t, side).start()
+
+    def stage_edges(t, planes):
+        for x in planes:
             for zb in range(nzb):
                 for c in (0, 1):
                     slot = pl.ds(zb * 2 + c, 1)
                     edge_out[t, 0, x, slot] = field[t, zb, c, x + 1, pl.ds(TOP, 1)]
                     edge_out[t, 1, x, slot] = field[t, zb, c, x + 1, pl.ds(TOP + ny - 1, 1)]
+
+    def send_edges(t, group):
         for dy in (0, 1):
             @pl.when(has_y[dy])
             def _():
-                edge(t, dy).start()
-        for dx in (0, 1):
-            for dy in (0, 1):
-                @pl.when(has_x[dx] & has_y[dy])
-                def _():
-                    corner(t, dx, dy).start()
-
-    def receive_edges(t):
+                edge(t, dy, group).start()
+        for dy in (0, 1):
+            @pl.when(has_x[group] & has_y[dy])
+            def _():
+                corner(t, group, dy).start()
+
+    def receive_edges(t, group):
+        planes = (rim[CROSS],) if group == CROSS else tuple(early + i for i in range(nx - 1))
         for dy in (0, 1):
             @pl.when(has_y[1 - dy])
             def _():
-                edge(t, dy).wait_recv()
+                edge(t, dy, group).wait_recv()
                 row = (TOP + ny, TOP - 1)[dy]
-                for x in range(nx):
+                for x in planes:
                     for zb in range(nzb):
                         for c in (0, 1):
                             field[t, zb, c, x + 1, pl.ds(row, 1)] = edge_in[t, dy, x, pl.ds(zb * 2 + c, 1)]
 
-    def receive_faces(t):
-        for dx in (0, 1):
-            for dy in (0, 1):
-                @pl.when(has_x[1 - dx] & has_y[1 - dy])
-                def _():
-                    corner(t, dx, dy).wait_recv()
-                    row = (TOP + ny, TOP - 1)[dy]
-                    for zb in range(nzb):
-                        for c in (0, 1):
-                            field[t, zb, c, (nx + 1, 0)[dx], pl.ds(row, 1)] = corner_in[
-                                t, dx, dy, pl.ds(zb * 2 + c, 1)
-                            ]
-        for dx in (0, 1):
-            @pl.when(has_x[1 - dx])
+    def receive_face(t, side):
+        for dy in (0, 1):
+            @pl.when(has_x[side] & has_y[1 - dy])
             def _():
-                face(t, dx).wait_recv()
-
-    for dx in (0, 1):
-        @pl.when(has_x[dx])
+                corner(t, side, dy).wait_recv()
+                row = (TOP + ny, TOP - 1)[dy]
+                for zb in range(nzb):
+                    for c in (0, 1):
+                        field[t, zb, c, halo[side], pl.ds(row, 1)] = corner_in[
+                            t, side, dy, pl.ds(zb * 2 + c, 1)
+                        ]
+        @pl.when(has_x[side])
+        def _():
+            face(t, side).wait_recv()
+
+    pl.semaphore_wait(barrier, greeted)
+    for side in (CROSS, CHIP):
+        @pl.when(has_x[side])
         def _():
             for zb in range(nzb):
-                first_face(zb, dx).start()
+                first_face(zb, side).start()
     arrived("now")
-    send_edges(0)
+    stage_edges(0, range(nx))
+    for group in (CHIP, CROSS):
+        send_edges(0, group)
 
     arrived("angle")
     arrived("params")
@@ -413,29 +424,40 @@
                     sums[zb, i, x, rows] = terms[i] if t == 0 else sums[zb, i, x, rows] + terms[i]
 
     half = nx // 2
-    inner, outer = list(range(1, nx - 1)), [0, nx - 1]
+
+    def onward(x):
+        return jnp.where(x < half, up, down)
+
+    def back(x):
+        return jnp.where(x < half, down, up)
 
     def far(x):
-        way = 0 if x < half else 1
         return pltpu.make_async_remote_copy(
             src_ref=sums.at[across, :, x],
             dst_ref=far_in.at[x],
             send_sem=fs.at[x],
             recv_sem=fr.at[x],
-            device_id={"src": (up, down)[way]},
+            device_id={"src": onward(x)},
             device_id_type=MESH,
         )
 
-    def near(x, way):
+    def near(x, peer, slot):
         return pltpu.make_async_remote_copy(
-            src_ref=sums.at[(up, down)[way], :, x],
-            dst_ref=near_in.at[way, x],
-            send_sem=ns.at[way, x],
-            recv_sem=nr.at[way, x],
-            device_id={"src": (up, down)[way]},
+            src_ref=sums.at[peer, :, x],
+            dst_ref=near_in.at[slot, x],
+            send_sem=ns.at[slot, x],
+            recv_sem=nr.at[slot, x],
+            device_id={"src": peer},
             device_id_type=MESH,
         )
 
+    def joined(x):
+        return near(x, onward(x), 0)
+
+    def single(x):
+        return near(x, back(x), 1)
+
+    order = [rim[CHIP] - sign * i for i in range(nx)]
     arrived("before")
     for t in range(steps):
         final = t == steps - 1
@@ -444,41 +466,34 @@
             operators(t, x)
             if final:
                 accumulate(t, x)
-
-        receive_edges(t)
-
-        @pl.loop(1, nx - 1)
-        def _(x):
-            plane(x)
-
-        if final:
-            for x in inner:
                 far(x).start()
-            for x in inner:
-                near(x, 1 if x < half else 0).start()
-        receive_faces(t)
+                single(x).start()
+
+        receive_edges(t, CHIP)
+        receive_face(t, CHIP)
+
+        @pl.loop(0, nx - 2)
+        def _(i):
+            plane(rim[CHIP] - sign * i)
+
+        receive_edges(t, CROSS)
+        plane(order[nx - 2])
         if not final:
-            @pl.loop(0, 2)
-            def _(i):
-                plane(i * (nx - 1))
-
-            send_faces(t + 1)
-            send_edges(t + 1)
+            send_face(t + 1, CHIP)
+            stage_edges(t + 1, order[: nx - 1])
+            send_edges(t + 1, CHIP)
+        receive_face(t, CROSS)
+        plane(order[nx - 1])
+        if not final:
+            send_face(t + 1, CROSS)
+            stage_edges(t + 1, order[nx - 1 :])
+            send_edges(t + 1, CROSS)
             if t == 0:
                 arrived("forward")
 
             @pl.loop(0, nx)
             def _(x):
                 accumulate(t, x)
-        else:
-            @pl.loop(0, 2)
-            def _(i):
-                plane(i * (nx - 1))
-
-    for x in outer:
-        far(x).start()
-    for x in outer:
-        near(x, 1 if x < half else 0).start()
 
     @pl.loop(0, nx)
     def _(x):
@@ -487,17 +502,16 @@
 
     out_copy = pltpu.make_async_copy(result, next_hbm.at[0], out_sem.at[0])
     out_copy.start()
-    for x in inner + outer:
-        way = 0 if x < half else 1
+    for x in order:
         far(x).wait_recv()
         for i in range(3):
-            sums[(up, down)[way], i, x] = sums[(up, down)[way], i, x] + far_in[x, i]
-        near(x, way).start()
+            sums[onward(x), i, x] = sums[onward(x), i, x] + far_in[x, i]
+        joined(x).start()
 
     arrived("own")
-    for x in inner + outer:
-        for way in (0, 1):
-            near(x, way).wait_recv()
+    for x in order:
+        single(x).wait_recv()
+        joined(x).wait_recv()
         for tile in range(tiles):
             rows = pl.ds(tile * ROWS, ROWS)
             a, b, c = (
@@ -518,26 +532,48 @@
         copy.start()
 
     for t in range(steps):
-        for dx in (0, 1):
-            @pl.when(has_x[dx])
+        for side in (CROSS, CHIP):
+            @pl.when(has_x[side])
             def _():
-                face(t, dx).wait_send()
+                face(t, side).wait_send()
         for dy in (0, 1):
             @pl.when(has_y[dy])
             def _():
-                edge(t, dy).wait_send()
-        for dx in (0, 1):
-            for dy in (0, 1):
-                @pl.when(has_x[dx] & has_y[dy])
+                for group in (CROSS, CHIP):
+                    edge(t, dy, group).wait_send()
+            for side in (CROSS, CHIP):
+                @pl.when(has_x[side] & has_y[dy])
                 def _():
-                    corner(t, dx, dy).wait_send()
+                    corner(t, side, dy).wait_send()
     for x in range(nx):
         far(x).wait_send()
-        for way in (0, 1):
-            near(x, way).wait_send()
+        joined(x).wait_send()
+        single(x).wait_send()
     out_copy.wait()
     for copy in grad_copies:
         copy.wait()
+
+
+def copy_kernel(*refs):
+    count = (len(refs) - 1) // 2
+    copies = [pltpu.make_async_copy(refs[i], refs[count + i], refs[-1].at[i]) for i in range(count)]
+    for copy in copies:
+        copy.start()
+    for copy in copies:
+        copy.wait()
+
+
+def hand_out(results):
+    anywhere = pl.BlockSpec(memory_space=pl.ANY)
+    return pl.pallas_call(
+        copy_kernel,
+        name="hand_out",
+        out_shape=tuple(jax.ShapeDtypeStruct(r.shape, r.dtype) for r in results),
+        in_specs=[anywhere] * len(results),
+        out_specs=(anywhere,) * len(results),
+        scratch_shapes=[pltpu.SemaphoreType.DMA((len(results),))],
+        compiler_params=pltpu.CompilerParams(vmem_limit_bytes=60 * 1024 * 1024),
+    )(*results)
 
 
 def on_device(
@@ -561,7 +597,7 @@
     block = jax.ShapeDtypeStruct((nx, ny, LANES), F32)
     anywhere = pl.BlockSpec(memory_space=pl.ANY)
     dma = pltpu.SemaphoreType.DMA
-    return pl.pallas_call(
+    results = pl.pallas_call(
         functools.partial(kernel, size_x, size_y, size_s, ny * size_y),
         name="adjoint_steps",
         out_shape=(jax.ShapeDtypeStruct(adjoint_now.shape, F32), block, block, block),
@@ -592,8 +628,8 @@
             dma((4,)),
             dma((steps, 2)),
             dma((steps, 2)),
-            dma((steps, 2)),
-            dma((steps, 2)),
+            dma((steps, 2, 2)),
+            dma((steps, 2, 2)),
             dma((steps, 2, 2)),
             dma((steps, 2, 2)),
             dma((nx,)),
@@ -602,7 +638,7 @@
             dma((2, nx)),
         ],
         compiler_params=pltpu.CompilerParams(
-            collective_id=0, has_side_effects=True, vmem_limit_bytes=48 * 1024 * 1024
+            collective_id=0, has_side_effects=True, vmem_limit_bytes=60 * 1024 * 1024
         ),
     )(
         adjoint_now,
@@ -615,8 +651,9 @@
         azimuth_level,
         channel_cell,
         channel_count,
-        residual_trace,
+        jnp.transpose(residual_trace, (1, 0, 2)),
     )
+    return hand_out(results)
 
 
 def solution(mesh):

time: 53.2 us -> 63.4 us (1.19)
  Pallas kernels: 40.1 us -> 62 us
  local copies, waits for them, and re-layouts: 11.4 us -> 0 us
    pallas_call x0 -> x1, Pallas kernels: none -> 23 us  [hand_out(): pl.pallas_call(copy_kernel, name='hand_out', out_shape=tuple((jax.ShapeDt...]
    unnamed x23 -> x0, local copies, waits for them, and re-layouts: 11.4 us -> none
    pallas_call x1, Pallas kernels: 40.1 us -> 39 us  [on_device(): pl.pallas_call(functools.partial(kernel, size_x, size_y, size_s, ny * siz...]
where the time goes in v2:
time: 63.4 us; the launch traced here: 63.3 us
  Pallas kernels  62 us (98%)
  between operations  1.29 us (2%)
    pallas_call x1, Pallas kernels, on_device(): pl.pallas_call(functools.partial(kernel, size_x, size_y, size_s, ny * siz...  39 us
    pallas_call x1, Pallas kernels, hand_out(): pl.pallas_call(copy_kernel, name='hand_out', out_shape=tuple((jax.ShapeDt...  23 us

profile of v2, /device:TPU:32, one launch (start us, length us, event | category | flops | bytes accessed | tf_op | source)
XLA Modules:
  0.0 63.3 jit_solution(3462589392700529107)
XLA Ops:
  1.3 39.0 %adjoint_steps.1 = (f32[1,2,4,32,512]{4,3,2,1,0:T(8,128)}, f32[4,32,128]{2,1,0:T(8,128)}, f32[4,32,128]{2,1,0:T(8,128)}, f32[4,32,128]{2,1,0:T(8,128)}) custom-call(f32[1,2,4,32,512]{4,3,2,1,0:T(8,128)} %now_hbm.1, f32[1,2,4,32,512]{4,3,2,1,0:T(8,128)} %before_hbm.1, bf16[3,1,2,4,32,512]{5,4,3,2,1,0:T(8,128)(2,1)} %forward_hbm.1, f32[4,32,512]{2,1,0:T(8,128)} %vel_hbm.1, ...), custom_call_target="tpu_custom_call" | custom-call | tf_op jit(solution)/shard_map/adjoint_steps/pallas_call | solution.py:600
  40.3 23.0 %hand_out.1 = (f32[1,2,4,32,512]{4,3,2,1,0:T(8,128)}, f32[4,32,128]{2,1,0:T(8,128)}, f32[4,32,128]{2,1,0:T(8,128)}, f32[4,32,128]{2,1,0:T(8,128)}) custom-call(f32[1,2,4,32,512]{4,3,2,1,0:T(8,128)} %get-tuple-element.8.refs_0_, f32[4,32,128]{2,1,0:T(8,128)} %get-tuple-element.9.refs_1_, f32[4,32,128]{2,1,0:T(8,128)} %get-tuple-element.10.refs_2_, ...), custom_call_target="tpu_custom_call" | custom-call | tf_op jit(solution)/shard_map/hand_out/pallas_call | solution.py:568

commit v3 on v2

--- a/solution.py
+++ b/solution.py
@@ -555,23 +555,34 @@
 
 
 def copy_kernel(*refs):
-    count = (len(refs) - 1) // 2
-    copies = [pltpu.make_async_copy(refs[i], refs[count + i], refs[-1].at[i]) for i in range(count)]
-    for copy in copies:
-        copy.start()
-    for copy in copies:
-        copy.wait()
+    sources, targets, stages = refs[:4], refs[4:8], refs[8:12]
+    fetched, stored = refs[12:]
+    pieces = [(0, (0, c, x)) for c in (0, 1) for x in range(sources[0].shape[2])]
+    pieces += [(i, ()) for i in (1, 2, 3)]
+    fetches, stores = [], []
+    for slot, (i, at) in enumerate(pieces):
+        source, stage, target = (ref.at[at] if at else ref for ref in (sources[i], stages[i], targets[i]))
+        fetches.append(pltpu.make_async_copy(source, stage, fetched.at[slot]))
+        stores.append(pltpu.make_async_copy(stage, target, stored.at[slot]))
+    for fetch in fetches:
+        fetch.start()
+    for fetch, store in zip(fetches, stores):
+        fetch.wait()
+        store.start()
+    for store in stores:
+        store.wait()
 
 
 def hand_out(results):
     anywhere = pl.BlockSpec(memory_space=pl.ANY)
+    pieces = 2 * results[0].shape[2] + 3
     return pl.pallas_call(
         copy_kernel,
         name="hand_out",
         out_shape=tuple(jax.ShapeDtypeStruct(r.shape, r.dtype) for r in results),
         in_specs=[anywhere] * len(results),
         out_specs=(anywhere,) * len(results),
-        scratch_shapes=[pltpu.SemaphoreType.DMA((len(results),))],
+        scratch_shapes=[pltpu.VMEM(r.shape, r.dtype) for r in results] + [pltpu.SemaphoreType.DMA((pieces,))] * 2,
         compiler_params=pltpu.CompilerParams(vmem_limit_bytes=60 * 1024 * 1024),
     )(*results)
 

time: 63.4 us -> 42.4 us (0.67)
  Pallas kernels: 62 us -> 41 us
    pallas_call x1, Pallas kernels: 23 us -> 1.96 us  [hand_out(): pl.pallas_call(copy_kernel, name='hand_out', out_shape=tuple((jax.ShapeDt...]
where the time goes in v3:
time: 42.4 us; the launch traced here: 42.3 us
  Pallas kernels  41 us (97%)
  between operations  1.29 us (3%)
    pallas_call x1, Pallas kernels, on_device(): pl.pallas_call(functools.partial(kernel, size_x, size_y, size_s, ny * siz...  39 us
    pallas_call x1, Pallas kernels, hand_out(): pl.pallas_call(copy_kernel, name='hand_out', out_shape=tuple((jax.ShapeDt...  1.96 us

profile of v3, /device:TPU:32, one launch (start us, length us, event | category | flops | bytes accessed | tf_op | source)
XLA Modules:
  0.0 42.3 jit_solution(3937404226859399350)
XLA Ops:
  1.3 39.0 %adjoint_steps.1 = (f32[1,2,4,32,512]{4,3,2,1,0:T(8,128)}, f32[4,32,128]{2,1,0:T(8,128)}, f32[4,32,128]{2,1,0:T(8,128)}, f32[4,32,128]{2,1,0:T(8,128)}) custom-call(f32[1,2,4,32,512]{4,3,2,1,0:T(8,128)} %now_hbm.1, f32[1,2,4,32,512]{4,3,2,1,0:T(8,128)} %before_hbm.1, bf16[3,1,2,4,32,512]{5,4,3,2,1,0:T(8,128)(2,1)} %forward_hbm.1, f32[4,32,512]{2,1,0:T(8,128)} %vel_hbm.1, ...), custom_call_target="tpu_custom_call" | custom-call | tf_op jit(solution)/shard_map/adjoint_steps/pallas_call | solution.py:611
  40.3 2.0 %hand_out.1 = (f32[1,2,4,32,512]{4,3,2,1,0:T(8,128)}, f32[4,32,128]{2,1,0:T(8,128)}, f32[4,32,128]{2,1,0:T(8,128)}, f32[4,32,128]{2,1,0:T(8,128)}) custom-call(f32[1,2,4,32,512]{4,3,2,1,0:T(8,128)} %get-tuple-element.8.refs_0_, f32[4,32,128]{2,1,0:T(8,128)} %get-tuple-element.9.refs_1_, f32[4,32,128]{2,1,0:T(8,128)} %get-tuple-element.10.refs_2_, ...), custom_call_target="tpu_custom_call" | custom-call | tf_op jit(solution)/shard_map/hand_out/pallas_call | solution.py:579

commit v4 on v3

--- a/solution.py
+++ b/solution.py
@@ -48,6 +48,7 @@
     field,
     before,
     forward,
+    wide,
     params,
     levels,
     own,
@@ -232,15 +233,17 @@
                     edge_out[t, 0, x, slot] = field[t, zb, c, x + 1, pl.ds(TOP, 1)]
                     edge_out[t, 1, x, slot] = field[t, zb, c, x + 1, pl.ds(TOP + ny - 1, 1)]
 
+    def send_corners(t, side):
+        for dy in (0, 1):
+            @pl.when(has_x[side] & has_y[dy])
+            def _():
+                corner(t, side, dy).start()
+
     def send_edges(t, group):
         for dy in (0, 1):
             @pl.when(has_y[dy])
             def _():
                 edge(t, dy, group).start()
-        for dy in (0, 1):
-            @pl.when(has_x[group] & has_y[dy])
-            def _():
-                corner(t, group, dy).start()
 
     def receive_edges(t, group):
         planes = (rim[CROSS],) if group == CROSS else tuple(early + i for i in range(nx - 1))
@@ -269,16 +272,18 @@
         def _():
             face(t, side).wait_recv()
 
+    arrived("now")
+    stage_edges(0, range(nx))
     pl.semaphore_wait(barrier, greeted)
+    send_corners(0, CROSS)
     for side in (CROSS, CHIP):
         @pl.when(has_x[side])
         def _():
             for zb in range(nzb):
                 first_face(zb, side).start()
-    arrived("now")
-    stage_edges(0, range(nx))
     for group in (CHIP, CROSS):
         send_edges(0, group)
+    send_corners(0, CHIP)
 
     arrived("angle")
     arrived("params")
@@ -408,8 +413,34 @@
                 out = stencil(t, c, x, tile, weights)
                 for zb in range(nzb):
                     ha[c, x, zb, rows] = out[zb]
-            if t < steps - 1:
-                advance(t, x, tile)
+            advance(t, x, tile)
+
+    parts_of = (tuple(range(1, tiles - 1)), (0, tiles - 1))
+    depth_of = ny // 2
+
+    def place(tile):
+        return pl.ds((parts_of[0] + parts_of[1]).index(tile) * ROWS, ROWS)
+
+    def widen(x):
+        for zb in range(nzb):
+            for c in (0, 1):
+                wide[c, x, zb] = forward[steps - 1, c, x, :, lanes_of(zb)].astype(F32)
+
+    def finish(x, part):
+        t = steps - 1
+        for tile in parts_of[part]:
+            rows = pl.ds(tile * ROWS, ROWS)
+            weights = [[coef[i, x, zb, rows] for i in range(6)] for zb in range(nzb)]
+            horiz, axial = (stencil(t, c, x, tile, weights) for c in (0, 1))
+            for zb in range(nzb):
+                ha[0, x, zb, rows] = horiz[zb]
+                ha[1, x, zb, rows] = axial[zb]
+                pf, qf = wide[0, x, zb, rows], wide[1, x, zb, rows]
+                terms = (pf * horiz[zb], pf * axial[zb] + qf * horiz[zb], qf * axial[zb])
+                for i in range(3):
+                    sums[zb, i, x, place(tile)] = sums[zb, i, x, place(tile)] + terms[i]
+        far(x, part).start()
+        single(x, part).start()
 
     def accumulate(t, x):
         for half in range(ny // 16):
@@ -421,7 +452,10 @@
                 qf = forward[t, 1, x, rows, cols].astype(F32)
                 terms = (pf * horiz, pf * axial + qf * horiz, qf * axial)
                 for i in range(3):
-                    sums[zb, i, x, rows] = terms[i] if t == 0 else sums[zb, i, x, rows] + terms[i]
+                    for j in (0, 1):
+                        spot = place(2 * half + j)
+                        term = terms[i][j * ROWS : (j + 1) * ROWS]
+                        sums[zb, i, x, spot] = term if t == 0 else sums[zb, i, x, spot] + term
 
     half = nx // 2
 
@@ -431,69 +465,86 @@
     def back(x):
         return jnp.where(x < half, down, up)
 
-    def far(x):
+    def rows_of(part):
+        return pl.ds(part * depth_of, depth_of)
+
+    def far(x, part):
         return pltpu.make_async_remote_copy(
-            src_ref=sums.at[across, :, x],
-            dst_ref=far_in.at[x],
-            send_sem=fs.at[x],
-            recv_sem=fr.at[x],
+            src_ref=sums.at[across, :, x, rows_of(part)],
+            dst_ref=far_in.at[part, x],
+            send_sem=fs.at[part, x],
+            recv_sem=fr.at[part, x],
             device_id={"src": onward(x)},
             device_id_type=MESH,
         )
 
-    def near(x, peer, slot):
+    def near(x, part, peer, slot):
         return pltpu.make_async_remote_copy(
-            src_ref=sums.at[peer, :, x],
-            dst_ref=near_in.at[slot, x],
-            send_sem=ns.at[slot, x],
-            recv_sem=nr.at[slot, x],
+            src_ref=sums.at[peer, :, x, rows_of(part)],
+            dst_ref=near_in.at[slot, part, x],
+            send_sem=ns.at[slot, part, x],
+            recv_sem=nr.at[slot, part, x],
             device_id={"src": peer},
             device_id_type=MESH,
         )
 
-    def joined(x):
-        return near(x, onward(x), 0)
-
-    def single(x):
-        return near(x, back(x), 1)
+    def joined(x, part):
+        return near(x, part, onward(x), 0)
+
+    def single(x, part):
+        return near(x, part, back(x), 1)
 
     order = [rim[CHIP] - sign * i for i in range(nx)]
     arrived("before")
-    for t in range(steps):
-        final = t == steps - 1
-
-        def plane(x):
-            operators(t, x)
-            if final:
-                accumulate(t, x)
-                far(x).start()
-                single(x).start()
-
+    for t in range(steps - 1):
         receive_edges(t, CHIP)
         receive_face(t, CHIP)
 
         @pl.loop(0, nx - 2)
         def _(i):
-            plane(rim[CHIP] - sign * i)
+            operators(t, rim[CHIP] - sign * i)
 
         receive_edges(t, CROSS)
-        plane(order[nx - 2])
-        if not final:
-            send_face(t + 1, CHIP)
-            stage_edges(t + 1, order[: nx - 1])
-            send_edges(t + 1, CHIP)
+        operators(t, order[nx - 2])
+        stage_edges(t + 1, order[: nx - 1])
+        send_face(t + 1, CHIP)
+        send_edges(t + 1, CHIP)
+        send_corners(t + 1, CHIP)
+        if t == 0:
+            arrived("forward")
+
+        @pl.loop(0, nx - 1)
+        def _(i):
+            accumulate(t, rim[CHIP] - sign * i)
+
+        if t == steps - 2:
+            finish(order[1], 0)
         receive_face(t, CROSS)
-        plane(order[nx - 1])
-        if not final:
-            send_face(t + 1, CROSS)
-            stage_edges(t + 1, order[nx - 1 :])
-            send_edges(t + 1, CROSS)
-            if t == 0:
-                arrived("forward")
-
+        operators(t, order[nx - 1])
+        stage_edges(t + 1, order[nx - 1 :])
+        send_corners(t + 1, CROSS)
+        send_face(t + 1, CROSS)
+        send_edges(t + 1, CROSS)
+        accumulate(t, order[nx - 1])
+        if t == 0:
             @pl.loop(0, nx)
             def _(x):
-                accumulate(t, x)
+                widen(x)
+
+    final = steps - 1
+    finish(order[2], 0)
+    receive_face(final, CHIP)
+    finish(order[0], 0)
+    receive_edges(final, CHIP)
+    finish(order[0], 1)
+    finish(order[1], 1)
+    receive_edges(final, CROSS)
+    finish(order[2], 1)
+    receive_face(final, CROSS)
+    finish(order[3], 0)
+    finish(order[3], 1)
+    sequence = [(1, 0), (2, 0), (0, 0), (0, 1), (1, 1), (2, 1), (3, 0), (3, 1)]
+    sequence = [(order[i], part) for i, part in sequence]
 
     @pl.loop(0, nx)
     def _(x):
@@ -502,20 +553,23 @@
 
     out_copy = pltpu.make_async_copy(result, next_hbm.at[0], out_sem.at[0])
     out_copy.start()
-    for x in order:
-        far(x).wait_recv()
+    for x, part in sequence:
+        far(x, part).wait_recv()
         for i in range(3):
-            sums[onward(x), i, x] = sums[onward(x), i, x] + far_in[x, i]
-        joined(x).start()
+            here = sums.at[onward(x), i, x, rows_of(part)]
+            here[...] = here[...] + far_in[part, x, i]
+        joined(x, part).start()
 
     arrived("own")
-    for x in order:
-        single(x).wait_recv()
-        joined(x).wait_recv()
-        for tile in range(tiles):
+    for x, part in sequence:
+        single(x, part).wait_recv()
+        joined(x, part).wait_recv()
+        for j, tile in enumerate(parts_of[part]):
             rows = pl.ds(tile * ROWS, ROWS)
+            spot = pl.ds(j * ROWS, ROWS)
             a, b, c = (
-                sums[me, i, x, rows] + near_in[0, x, i, rows] + near_in[1, x, i, rows] for i in range(3)
+                sums[me, i, x, place(tile)] + near_in[0, part, x, i, spot] + near_in[1, part, x, i, spot]
+                for i in range(3)
             )
             vel = own[0, x, rows]
             stretch = 1.0 + 2.0 * own[1, x, rows]
@@ -545,10 +599,10 @@
                 @pl.when(has_x[side] & has_y[dy])
                 def _():
                     corner(t, side, dy).wait_send()
-    for x in range(nx):
-        far(x).wait_send()
-        joined(x).wait_send()
-        single(x).wait_send()
+    for x, part in sequence:
+        far(x, part).wait_send()
+        joined(x, part).wait_send()
+        single(x, part).wait_send()
     out_copy.wait()
     for copy in grad_copies:
         copy.wait()
@@ -618,6 +672,7 @@
             pltpu.VMEM((steps, nzb, 2, nx + 2, ny + 2 * TOP, LANES), F32),
             pltpu.VMEM((2, nx, ny, depth), F32),
             pltpu.VMEM((steps, 2, nx, ny, depth), BF16),
+            pltpu.VMEM((2, nx, nzb, ny, LANES), F32),
             pltpu.VMEM((3, nx, ny, depth), F32),
             pltpu.VMEM((2, nx, ny, depth), jnp.int32),
             pltpu.VMEM((3, nx, ny, LANES), F32),
@@ -631,8 +686,8 @@
             pltpu.VMEM((steps, 2, nx, 2 * nzb, LANES), F32),
             pltpu.VMEM((steps, 2, nx, 2 * nzb, LANES), F32),
             pltpu.VMEM((steps, 2, 2, 2 * nzb, LANES), F32),
-            pltpu.VMEM((nx, 3, ny, LANES), F32),
-            pltpu.VMEM((2, nx, 3, ny, LANES), F32),
+            pltpu.VMEM((2, nx, 3, ny // 2, LANES), F32),
+            pltpu.VMEM((2, 2, nx, 3, ny // 2, LANES), F32),
             pltpu.VMEM((2, nx, ny, depth), F32),
             pltpu.VMEM((3, nx, ny, LANES), F32),
             dma((nzb + 12,)),
@@ -643,10 +698,10 @@
             dma((steps, 2, 2)),
             dma((steps, 2, 2)),
             dma((steps, 2, 2)),
-            dma((nx,)),
-            dma((nx,)),
             dma((2, nx)),
             dma((2, nx)),
+            dma((2, 2, nx)),
+            dma((2, 2, nx)),
         ],
         compiler_params=pltpu.CompilerParams(
             collective_id=0, has_side_effects=True, vmem_limit_bytes=60 * 1024 * 1024

time: 42.4 us -> 40.5 us (0.955)
  Pallas kernels: 41 us -> 39.1 us
    pallas_call x1, Pallas kernels: 39 us -> 37.1 us  [on_device(): pl.pallas_call(functools.partial(kernel, size_x, size_y, size_s, ny * siz...]
where the time goes in v4:
time: 40.5 us; the launch traced here: 40.4 us
  Pallas kernels  39.1 us (97%)
  between operations  1.29 us (3%)
    pallas_call x1, Pallas kernels, on_device(): pl.pallas_call(functools.partial(kernel, size_x, size_y, size_s, ny * siz...  37.1 us
    pallas_call x1, Pallas kernels, hand_out(): pl.pallas_call(copy_kernel, name='hand_out', out_shape=tuple((jax.ShapeDt...  1.96 us

profile of v4, /device:TPU:32, one launch (start us, length us, event | category | flops | bytes accessed | tf_op | source)
XLA Modules:
  0.0 40.4 jit_solution(1419853451614290204)
XLA Ops:
  1.3 37.1 %adjoint_steps.1 = (f32[1,2,4,32,512]{4,3,2,1,0:T(8,128)}, f32[4,32,128]{2,1,0:T(8,128)}, f32[4,32,128]{2,1,0:T(8,128)}, f32[4,32,128]{2,1,0:T(8,128)}) custom-call(f32[1,2,4,32,512]{4,3,2,1,0:T(8,128)} %now_hbm.1, f32[1,2,4,32,512]{4,3,2,1,0:T(8,128)} %before_hbm.1, bf16[3,1,2,4,32,512]{5,4,3,2,1,0:T(8,128)(2,1)} %forward_hbm.1, f32[4,32,512]{2,1,0:T(8,128)} %vel_hbm.1, ...), custom_call_target="tpu_custom_call" | custom-call | tf_op jit(solution)/shard_map/adjoint_steps/pallas_call | solution.py:665
  38.4 2.0 %hand_out.1 = (f32[1,2,4,32,512]{4,3,2,1,0:T(8,128)}, f32[4,32,128]{2,1,0:T(8,128)}, f32[4,32,128]{2,1,0:T(8,128)}, f32[4,32,128]{2,1,0:T(8,128)}) custom-call(f32[1,2,4,32,512]{4,3,2,1,0:T(8,128)} %get-tuple-element.8.refs_0_, f32[4,32,128]{2,1,0:T(8,128)} %get-tuple-element.9.refs_1_, f32[4,32,128]{2,1,0:T(8,128)} %get-tuple-element.10.refs_2_, ...), custom_call_target="tpu_custom_call" | custom-call | tf_op jit(solution)/shard_map/hand_out/pallas_call | solution.py:633

commit v5 on v4

--- a/solution.py
+++ b/solution.py
@@ -124,26 +124,12 @@
     load("own", nzb + 9, vel_hbm.at[:, :, mine], own.at[0])
     load("own", nzb + 10, eps_hbm.at[:, :, mine], own.at[1])
     load("own", nzb + 11, delta_hbm.at[:, :, mine], own.at[2])
-    for group in loads.values():
-        for copy in group:
-            copy.start()
-
     def arrived(name):
         for copy in loads[name]:
             copy.wait()
 
     barrier = pltpu.get_barrier_semaphore()
     greeted = jnp.int32(2)
-    for side in (CROSS, CHIP):
-        @pl.when(has_x[side])
-        def _():
-            pl.semaphore_signal(barrier, inc=1, device_id={"gx": to_x[side]}, device_id_type=MESH)
-        greeted = greeted + has_x[side].astype(jnp.int32)
-    for dy in (0, 1):
-        @pl.when(has_y[dy])
-        def _():
-            pl.semaphore_signal(barrier, inc=1, device_id={"gy": to_y[dy]}, device_id_type=MESH)
-        greeted = greeted + has_y[dy].astype(jnp.int32)
     for side in (CROSS, CHIP):
         for dy in (0, 1):
             both = has_x[side] & has_y[dy]
@@ -155,6 +141,20 @@
             greeted = greeted + both.astype(jnp.int32)
     for peer in (up, down):
         pl.semaphore_signal(barrier, inc=1, device_id={"src": peer}, device_id_type=MESH)
+    for side in (CROSS, CHIP):
+        @pl.when(has_x[side])
+        def _():
+            pl.semaphore_signal(barrier, inc=1, device_id={"gx": to_x[side]}, device_id_type=MESH)
+        greeted = greeted + has_x[side].astype(jnp.int32)
+    for dy in (0, 1):
+        @pl.when(has_y[dy])
+        def _():
+            pl.semaphore_signal(barrier, inc=1, device_id={"gy": to_y[dy]}, device_id_type=MESH)
+        greeted = greeted + has_y[dy].astype(jnp.int32)
+
+    for group in loads.values():
+        for copy in group:
+            copy.start()
 
     for side in (CROSS, CHIP):
         @pl.when(jnp.logical_not(has_x[side]))
@@ -285,6 +285,17 @@
         send_edges(0, group)
     send_corners(0, CHIP)
 
+    lane = lax.broadcasted_iota(jnp.int32, (ROWS, LANES), 1)
+    first, last = lane == 0, lane == LANES - 1
+    zero = jnp.zeros((ROWS, LANES), F32)
+
+    def shifted(blocks):
+        ahead = [pltpu.roll(block, LANES - 1, 1) for block in blocks] + [zero]
+        behind = [zero] + [pltpu.roll(block, 1, 1) for block in blocks]
+        after = [jnp.where(last, ahead[i + 1], ahead[i]) for i in range(nzb)]
+        prior = [jnp.where(first, behind[i], behind[i + 1]) for i in range(nzb)]
+        return after, prior
+
     arrived("angle")
     arrived("params")
 
@@ -292,6 +303,7 @@
     def _(x):
         for tile in range(tiles):
             rows = pl.ds(tile * ROWS, ROWS)
+            deep = ([], [], [])
             for zb in range(nzb):
                 cols = lanes_of(zb)
                 tilt = levels[0, x, rows, cols].astype(F32)
@@ -306,14 +318,18 @@
                 slope = 0.5 * sin_t * cos_t
                 coef[0, x, zb, rows] = flat * cos_p * cos_p
                 coef[1, x, zb, rows] = flat * sin_p * sin_p
-                coef[2, x, zb, rows] = cos_t * cos_t
                 coef[3, x, zb, rows] = 0.5 * flat * sin_p * cos_p
-                coef[4, x, zb, rows] = slope * sin_p
-                coef[5, x, zb, rows] = slope * cos_p
+                for weight, value in zip(deep, (cos_t * cos_t, slope * sin_p, slope * cos_p)):
+                    weight.append(value)
                 vel = params[0, x, rows, cols]
                 coef[6, x, zb, rows] = vel * vel
                 coef[7, x, zb, rows] = 1.0 + 2.0 * params[1, x, rows, cols]
                 coef[8, x, zb, rows] = jnp.sqrt(1.0 + 2.0 * params[2, x, rows, cols])
+            for slot, weight in zip((2, 4, 5), deep):
+                after, prior = shifted(weight)
+                for zb in range(nzb):
+                    coef[slot, x, zb, rows] = prior[zb]
+                    coef[{2: 9, 4: 10, 5: 11}[slot], x, zb, rows] = after[zb]
 
     arrived("channels")
     cell = cells[...]
@@ -341,17 +357,6 @@
         moved = table if t == 0 else pltpu.roll(table, LANES - t, 1)
         surf[t] = jnp.where(spot_lane == 0, moved, 0.0)
 
-    lane = lax.broadcasted_iota(jnp.int32, (ROWS, LANES), 1)
-    first, last = lane == 0, lane == LANES - 1
-    zero = jnp.zeros((ROWS, LANES), F32)
-
-    def shifted(blocks):
-        ahead = [pltpu.roll(block, LANES - 1, 1) for block in blocks] + [zero]
-        behind = [zero] + [pltpu.roll(block, 1, 1) for block in blocks]
-        after = [jnp.where(last, ahead[i + 1], ahead[i]) for i in range(nzb)]
-        prior = [jnp.where(first, behind[i], behind[i + 1]) for i in range(nzb)]
-        return after, prior
-
     def stencil(t, c, x, tile, weights):
         def read(dx, dy):
             rows = pl.ds(TOP + tile * ROWS + dy, ROWS)
@@ -361,28 +366,27 @@
         slope_y = [a - b for a, b in zip(north, south)]
         slope_x = [a - b for a, b in zip(right, left)]
         cross = [(a - b) - (d - e) for a, b, d, e in zip(read(1, 1), read(1, -1), read(-1, 1), read(-1, -1))]
-        after, prior = shifted(center)
-        after_y, prior_y = shifted(slope_y)
-        after_x, prior_x = shifted(slope_x)
+        onto_prior, onto_after = [], []
+        for zb in range(nzb):
+            w, v = weights[zb], center[zb]
+            ahead = w[2] * v + w[4] * slope_y[zb] + w[5] * slope_x[zb]
+            behind = w[6] * v - w[7] * slope_y[zb] - w[8] * slope_x[zb]
+            onto_prior.append(v - ahead if c == 0 else ahead)
+            onto_after.append(v - behind if c == 0 else behind)
+        after, _ = shifted(onto_prior)
+        _, prior = shifted(onto_after)
         out = []
         for zb in range(nzb):
             w = weights[zb]
             sum_x = right[zb] + left[zb]
             sum_y = north[zb] + south[zb]
-            sum_z = after[zb] + prior[zb]
-            mixed = (
-                w[0] * sum_x
-                + w[1] * sum_y
-                + w[2] * sum_z
-                + w[3] * cross[zb]
-                + w[4] * (after_y[zb] - prior_y[zb])
-                + w[5] * (after_x[zb] - prior_x[zb])
-            )
+            mixed = w[0] * sum_x + w[1] * sum_y + w[3] * cross[zb]
+            deep = after[zb] + prior[zb]
             twice = center[zb] + center[zb]
             if c == 0:
-                out.append((sum_x + sum_y + sum_z) - (twice + twice) - mixed)
+                out.append((sum_x + sum_y) - (twice + twice) - mixed + deep)
             else:
-                out.append(mixed - twice)
+                out.append(mixed - twice + deep)
         return out
 
     def advance(t, x, tile):
@@ -408,7 +412,7 @@
     def operators(t, x):
         for tile in range(tiles):
             rows = pl.ds(tile * ROWS, ROWS)
-            weights = [[coef[i, x, zb, rows] for i in range(6)] for zb in range(nzb)]
+            weights = [[coef[i, x, zb, rows] for i in (0, 1, 2, 3, 4, 5, 9, 10, 11)] for zb in range(nzb)]
             for c in (0, 1):
                 out = stencil(t, c, x, tile, weights)
                 for zb in range(nzb):
@@ -416,10 +420,10 @@
             advance(t, x, tile)
 
     parts_of = (tuple(range(1, tiles - 1)), (0, tiles - 1))
-    depth_of = ny // 2
 
     def place(tile):
-        return pl.ds((parts_of[0] + parts_of[1]).index(tile) * ROWS, ROWS)
+        part = 0 if tile in parts_of[0] else 1
+        return part, pl.ds(parts_of[part].index(tile) * ROWS, ROWS)
 
     def widen(x):
         for zb in range(nzb):
@@ -430,7 +434,7 @@
         t = steps - 1
         for tile in parts_of[part]:
             rows = pl.ds(tile * ROWS, ROWS)
-            weights = [[coef[i, x, zb, rows] for i in range(6)] for zb in range(nzb)]
+            weights = [[coef[i, x, zb, rows] for i in (0, 1, 2, 3, 4, 5, 9, 10, 11)] for zb in range(nzb)]
             horiz, axial = (stencil(t, c, x, tile, weights) for c in (0, 1))
             for zb in range(nzb):
                 ha[0, x, zb, rows] = horiz[zb]
@@ -438,7 +442,8 @@
                 pf, qf = wide[0, x, zb, rows], wide[1, x, zb, rows]
                 terms = (pf * horiz[zb], pf * axial[zb] + qf * horiz[zb], qf * axial[zb])
                 for i in range(3):
-                    sums[zb, i, x, place(tile)] = sums[zb, i, x, place(tile)] + terms[i]
+                    spot = place(tile)[1]
+                    sums[zb, part, x, i, spot] = sums[zb, part, x, i, spot] + terms[i]
         far(x, part).start()
         single(x, part).start()
 
@@ -453,9 +458,9 @@
                 terms = (pf * horiz, pf * axial + qf * horiz, qf * axial)
                 for i in range(3):
                     for j in (0, 1):
-                        spot = place(2 * half + j)
+                        part, spot = place(2 * half + j)
                         term = terms[i][j * ROWS : (j + 1) * ROWS]
-                        sums[zb, i, x, spot] = term if t == 0 else sums[zb, i, x, spot] + term
+                        sums[zb, part, x, i, spot] = term if t == 0 else sums[zb, part, x, i, spot] + term
 
     half = nx // 2
 
@@ -465,12 +470,9 @@
     def back(x):
         return jnp.where(x < half, down, up)
 
-    def rows_of(part):
-        return pl.ds(part * depth_of, depth_of)
-
     def far(x, part):
         return pltpu.make_async_remote_copy(
-            src_ref=sums.at[across, :, x, rows_of(part)],
+            src_ref=sums.at[across, part, x],
             dst_ref=far_in.at[part, x],
             send_sem=fs.at[part, x],
             recv_sem=fr.at[part, x],
@@ -480,7 +482,7 @@
 
     def near(x, part, peer, slot):
         return pltpu.make_async_remote_copy(
-            src_ref=sums.at[peer, :, x, rows_of(part)],
+            src_ref=sums.at[peer, part, x],
             dst_ref=near_in.at[slot, part, x],
             send_sem=ns.at[slot, part, x],
             recv_sem=nr.at[slot, part, x],
@@ -555,9 +557,8 @@
     out_copy.start()
     for x, part in sequence:
         far(x, part).wait_recv()
-        for i in range(3):
-            here = sums.at[onward(x), i, x, rows_of(part)]
-            here[...] = here[...] + far_in[part, x, i]
+        here = sums.at[onward(x), part, x]
+        here[...] = here[...] + far_in[part, x]
         joined(x, part).start()
 
     arrived("own")
@@ -568,7 +569,7 @@
             rows = pl.ds(tile * ROWS, ROWS)
             spot = pl.ds(j * ROWS, ROWS)
             a, b, c = (
-                sums[me, i, x, place(tile)] + near_in[0, part, x, i, spot] + near_in[1, part, x, i, spot]
+                sums[me, part, x, i, spot] + near_in[0, part, x, i, spot] + near_in[1, part, x, i, spot]
                 for i in range(3)
             )
             vel = own[0, x, rows]
@@ -679,10 +680,10 @@
             pltpu.VMEM((1, channels), jnp.int32),
             pltpu.VMEM((steps, channels), F32),
             pltpu.VMEM((LANES, channels), F32),
-            pltpu.VMEM((9, nx, nzb, ny, LANES), F32),
+            pltpu.VMEM((12, nx, nzb, ny, LANES), F32),
             pltpu.VMEM((steps, nx * ny, LANES), F32),
             pltpu.VMEM((2, nx, nzb, ny, LANES), F32),
-            pltpu.VMEM((nzb, 3, nx, ny, LANES), F32),
+            pltpu.VMEM((nzb, 2, nx, 3, ny // 2, LANES), F32),
             pltpu.VMEM((steps, 2, nx, 2 * nzb, LANES), F32),
             pltpu.VMEM((steps, 2, nx, 2 * nzb, LANES), F32),
             pltpu.VMEM((steps, 2, 2, 2 * nzb, LANES), F32),

time: 40.5 us -> 40.2 us (level)
  Pallas kernels: 39.1 us -> 38.5 us
    pallas_call x1, Pallas kernels: 37.1 us -> 36.5 us  [on_device(): pl.pallas_call(functools.partial(kernel, size_x, size_y, size_s, ny * siz...]
where the time goes in v5:
time: 40.2 us; the launch traced here: 39.8 us
  Pallas kernels  38.5 us (96%)
  between operations  1.29 us (3%)
    pallas_call x1, Pallas kernels, on_device(): pl.pallas_call(functools.partial(kernel, size_x, size_y, size_s, ny * siz...  36.5 us
    pallas_call x1, Pallas kernels, hand_out(): pl.pallas_call(copy_kernel, name='hand_out', out_shape=tuple((jax.ShapeDt...  1.96 us

profile of v5, /device:TPU:32, one launch (start us, length us, event | category | flops | bytes accessed | tf_op | source)
XLA Modules:
  0.0 39.8 jit_solution(15304141675573923854)
XLA Ops:
  1.3 36.5 %adjoint_steps.1 = (f32[1,2,4,32,512]{4,3,2,1,0:T(8,128)}, f32[4,32,128]{2,1,0:T(8,128)}, f32[4,32,128]{2,1,0:T(8,128)}, f32[4,32,128]{2,1,0:T(8,128)}) custom-call(f32[1,2,4,32,512]{4,3,2,1,0:T(8,128)} %now_hbm.1, f32[1,2,4,32,512]{4,3,2,1,0:T(8,128)} %before_hbm.1, bf16[3,1,2,4,32,512]{5,4,3,2,1,0:T(8,128)(2,1)} %forward_hbm.1, f32[4,32,512]{2,1,0:T(8,128)} %vel_hbm.1, ...), custom_call_target="tpu_custom_call" | custom-call | tf_op jit(solution)/shard_map/adjoint_steps/pallas_call | solution.py:666
  37.8 2.0 %hand_out.1 = (f32[1,2,4,32,512]{4,3,2,1,0:T(8,128)}, f32[4,32,128]{2,1,0:T(8,128)}, f32[4,32,128]{2,1,0:T(8,128)}, f32[4,32,128]{2,1,0:T(8,128)}) custom-call(f32[1,2,4,32,512]{4,3,2,1,0:T(8,128)} %get-tuple-element.8.refs_0_, f32[4,32,128]{2,1,0:T(8,128)} %get-tuple-element.9.refs_1_, f32[4,32,128]{2,1,0:T(8,128)} %get-tuple-element.10.refs_2_, ...), custom_call_target="tpu_custom_call" | custom-call | tf_op jit(solution)/shard_map/hand_out/pallas_call | solution.py:634
